TPU v7x, 256 devices: a whole 4x4x8 slice. The times are simulated.
256 devices in a mesh: lon: 64 (over x_lo, y, z), lat: 4 (over x_hi, core).
Axes of the slice: x: 4 (x_hi: 2, x_lo: 2; x = x_hi * 2 + x_lo), y: 4, z: 8, core: 2. Of those that a mesh axis runs over, the one named last changes fastest.
Arguments:
- hidden_in: bfloat16 [8, 128, 1024, 512], P(None, None, 'lon', 'lat'), may hold values from -6 to 6
- w_conv1: bfloat16 [3, 3, 128, 128], replicated, may hold values from -0.1875 to 0.1875
- b_conv1: float32 [128], replicated, may hold values from -3 to 3
- w_conv2: bfloat16 [3, 3, 128, 12], replicated, may hold values from -0.1875 to 0.1875
- b_conv2: float32 [12], replicated, may hold values from -3.5 to 3.5
- state: float32 [6, 8, 1024, 512], P(None, None, 'lon', 'lat'), may hold values from -6 to 6
Outputs:
- velocity: float32 [12, 8, 1024, 512], P(None, None, 'lon', 'lat')
- tendency: float32 [6, 8, 1024, 512], P(None, None, 'lon', 'lat')
All inputs are finite; a program needn't handle non-finite values.
Results may differ from a plain program's by a relative error of at most 0.0013.
Values may be sent and summed in bfloat16 or wider, within the bound.
A program may use at most 128 MiB of HBM per device.

v0:
```python
import math

import jax
import jax.numpy as jnp
from jax import lax
from jax.sharding import PartitionSpec as P

time_step = 0.5
speed_cap = 0.6
cos_floor = 0.5


def padded_2(block, sides, width):
    for axis, dim in sides:
        count = lax.axis_size(axis)
        forward = [(i, i + 1) for i in range(count - 1)]
        forward.append((count - 1, 0))
        backward = [(target, source) for source, target in forward]
        low = lax.ppermute(
            lax.slice_in_dim(block, block.shape[dim] - width, None, axis=dim), axis, forward
        )
        high = lax.ppermute(lax.slice_in_dim(block, 0, width, axis=dim), axis, backward)
        block = jnp.concatenate([low, block, high], axis=dim)
    return block


def with_halo(array, sides, width):
    edges = {}
    for axis, dim in sides:
        peers, length = (lax.axis_size(axis), array.shape[dim])
        up = [(i, (i + 1) % peers) for i in range(peers)]
        last = lax.slice_in_dim(array, length - width, length, axis=dim)
        leading = lax.slice_in_dim(array, 0, width, axis=dim)
        edges[dim] = (
            lax.ppermute(last, axis, up),
            lax.ppermute(leading, axis, [(b, a) for a, b in up]),
        )
    done = []
    for _, dim in sides:
        low, high = edges[dim]
        around = [(width, width) if d in done else (0, 0) for d in range(array.ndim)]
        array = jnp.concatenate([jnp.pad(low, around), array, jnp.pad(high, around)], axis=dim)
        done.append(dim)
    return array


def crop(field, have, want):
    depth = have - want
    if depth == 0:
        return field
    return field[..., depth : field.shape[-2] - depth, depth : field.shape[-1] - depth]


def lat_profile(margin, lat_dev):
    n_lat = lat_dev * lax.axis_size("lat")
    global_rows = (
        lax.axis_index("lat") * lat_dev + jnp.arange(lat_dev + 2 * margin, dtype=jnp.int32) - margin
    )
    inside = ((global_rows >= 0) & (global_rows < n_lat)).astype(jnp.float32)
    latitude = (global_rows.astype(jnp.float32) + 0.5) * (math.pi / n_lat) - 0.5 * math.pi
    cosine = jnp.maximum(jnp.cos(latitude), cos_floor)
    return (inside, cosine, 1.0 / cosine)


def conv_block(padded, weight):
    out_x = padded.shape[1] - 2
    out_y = padded.shape[2] - 2
    taps = jnp.stack(
        [
            padded[:, row_off : row_off + out_x, col_off : col_off + out_y]
            for row_off in range(3)
            for col_off in range(3)
        ]
    )
    stacked = weight.reshape(9, weight.shape[2], weight.shape[3])
    return jnp.einsum("tcxy,tco->oxy", taps, stacked, preferred_element_type=jnp.float32)


def body(hidden_in, w_conv1, b_conv1, w_conv2, b_conv2, state):
    lat_dev = state.shape[3]
    reach = 1

    def first_layer(features):
        return jax.nn.silu(conv_block(features, w_conv1) + b_conv1[:, None, None]).astype(
            jnp.bfloat16
        )

    def second_layer(hidden):
        return speed_cap * jnp.tanh(conv_block(hidden, w_conv2) + b_conv2[:, None, None])

    in_width = reach + 2
    padded = padded_2(hidden_in, (("lon", 2), ("lat", 3)), in_width)
    padded = padded * lat_profile(in_width, lat_dev)[0].astype(jnp.bfloat16)
    hidden_keep = lat_profile(reach + 1, lat_dev)[0].astype(jnp.bfloat16)
    speed_keep = lat_profile(reach, lat_dev)[0]

    def level(features):
        hidden = first_layer(features) * hidden_keep
        return second_layer(hidden) * speed_keep

    wide = jnp.transpose(lax.map(level, padded), (1, 0, 2, 3))
    velocity = crop(wide, reach, 0)
    zonal_wide = wide[0::2]
    north_wide = wide[1::2]
    cosine_wide = lat_profile(reach, lat_dev)[1]
    flux = north_wide * cosine_wide
    metric_rows = lat_profile(reach - 1, lat_dev)[2]
    divergence = metric_rows * (
        (zonal_wide[..., 2:, 1:-1] - zonal_wide[..., :-2, 1:-1]) * 0.5
        + (flux[..., 1:-1, 2:] - flux[..., 1:-1, :-2]) * 0.5
    )
    zonal_in = crop(zonal_wide, reach, reach - 1)
    north_in = crop(north_wide, reach, reach - 1)

    def section_rate(q_padded, margin_in):
        margin_out = margin_in - 1
        zonal = crop(zonal_in, reach - 1, margin_out)
        north = crop(north_in, reach - 1, margin_out)
        spread = crop(divergence, reach - 1, margin_out)
        centre = q_padded[..., 1:-1, 1:-1]
        back_x = centre - q_padded[..., :-2, 1:-1]
        fore_x = q_padded[..., 2:, 1:-1] - centre
        back_y = centre - q_padded[..., 1:-1, :-2]
        fore_y = q_padded[..., 1:-1, 2:] - centre
        advect = (
            metric_rows * (jnp.maximum(zonal, 0.0) * back_x + jnp.minimum(zonal, 0.0) * fore_x)
            + jnp.maximum(north, 0.0) * back_y
            + jnp.minimum(north, 0.0) * fore_y
        )
        return -(advect + centre * spread)

    keep_one = lat_profile(1, lat_dev)[0]

    def section_from(field):
        edged = with_halo(field, (("lon", 2), ("lat", 3)), 1) * keep_one
        return section_rate(edged, 1)

    rate_one = section_from(state)
    rate_two = section_from(state + 0.5 * time_step * rate_one)
    rate_three = section_from(state + 0.5 * time_step * rate_two)
    rate_four = section_from(state + time_step * rate_three)
    tendency = (rate_one + 2.0 * rate_two + 2.0 * rate_three + rate_four) / 6.0
    return (velocity, tendency)


def solution(mesh):
    placed = (P(None, None, "lon", "lat"), P(), P(), P(), P(), P(None, None, "lon", "lat"))
    return jax.shard_map(
        body,
        mesh=mesh,
        in_specs=placed,
        out_specs=(P(None, None, "lon", "lat"), P(None, None, "lon", "lat")),
        check_vma=False,
    )
```

profile of v0, /device:TPU:1, one launch (start us, length us, event | category | flops | bytes accessed | tf_op | source)
XLA Modules:
  0.0 190.4 jit_solution(5517449243793609967)
XLA Ops:
  0.6 6.8 %copy.17 = bf16[8,128,16,128]{1,3,2,0:T(8,128)(2,1)} copy(bf16[8,128,16,128]{3,2,1,0:T(8,128)(2,1)} %param.8) | data formatting | bytes 8388608 | tf_op args[0]
  7.4 2.4 %fusion.85 = (bf16[8,128,3,128]{1,3,2,0:T(8,128)(2,1)}, bf16[8,128,3,128]{1,3,2,0:T(8,128)(2,1)S(1)}) fusion(bf16[8,128,16,128]{1,3,2,0:T(8,128)(2,1)} %copy.17), kind=kLoop, calls=%fused_computation.151 | loop fusion | bytes 3145728 | tf_op jit(solution)/shard_map/slice | solution.py:20
  9.8 2.5 %collective-permute-start = (bf16[8,128,3,128]{1,3,2,0:T(8,128)(2,1)}, bf16[8,128,3,128]{1,3,2,0:T(8,128)(2,1)S(1)}, u32[]{:S(2)}, u32[]{:S(2)}) collective-permute-start(bf16[8,128,3,128]{1,3,2,0:T(8,128)(2,1)} %get-tuple-element.119), channel_id=1, source_target_pairs={{0,4},{4,8},{8,12},{12,16},{16,20},{20,24},{24,28},{28,32},{32,36}... | collective-permute-start | bytes 2359304 | tf_op jit(solution)/shard_map/ppermute | solution.py:19
  12.3 7.3 %collective-permute-start.1 = (bf16[8,128,3,128]{1,3,2,0:T(8,128)(2,1)S(1)}, bf16[8,128,3,128]{1,3,2,0:T(8,128)(2,1)S(1)}, u32[]{:S(2)}, u32[]{:S(2)}) collective-permute-start(bf16[8,128,3,128]{1,3,2,0:T(8,128)(2,1)S(1)} %get-tuple-element.120), channel_id=1, source_target_pairs={{4,0},{8,4},{12,8},{16,12},{20,16},{24,20},{28,24},{32,28},{36,32}... | collective-permute-start | bytes 2359304 | tf_op jit(solution)/shard_map/ppermute | solution.py:22
  19.8 3.4 %collective-permute-start.4 = (f32[6,8,16,1]{3,2,1,0:T(8,128)S(1)}, f32[6,8,16,1]{3,2,1,0:T(8,128)}, u32[]{:S(2)}, u32[]{:S(2)}) collective-permute-start(f32[6,8,16,1]{3,2,1,0:T(8,128)S(1)} %get-tuple-element.138), channel_id=1, source_target_pairs={{0,1},{1,2},{2,3},{3,0},{4,5},{5,6},{6,7},{7,4},{8,9},{9,10},{10,1... | collective-permute-start | bytes 9224 | tf_op jit(solution)/shard_map/ppermute | solution.py:35
  24.0 13.2 %collective-permute-done = bf16[8,128,3,128]{1,3,2,0:T(8,128)(2,1)S(1)} collective-permute-done((bf16[8,128,3,128]{1,3,2,0:T(8,128)(2,1)}, bf16[8,128,3,128]{1,3,2,0:T(8,128)(2,1)S(1)}, u32[]{:S(2)}, u32[]{:S(2)}) %collective-permute-start) | collective-permute-done | bytes 786464 | tf_op jit(solution)/shard_map/ppermute | solution.py:19
  37.1 1.1 collective-permute-start.6
  38.3 1.3 pad_maximum_fusion.2
  39.6 4.5 %collective-permute-start.2 = (bf16[8,128,22,3]{1,3,2,0:T(4,128)(2,1)S(1)}, bf16[8,128,22,3]{1,3,2,0:T(4,128)(2,1)S(1)}, u32[]{:S(2)}, u32[]{:S(2)}) collective-permute-start(bf16[8,128,22,3]{1,3,2,0:T(4,128)(2,1)S(1)} %get-tuple-element.117), channel_id=1, source_target_pairs={{0,1},{1,2},{2,3},{3,0},{4,5},{5,6},{6,7},{7,4},{8,9},{9,10},{10,1... | collective-permute-start | bytes 405512 | tf_op jit(solution)/shard_map/ppermute | solution.py:19
  44.1 1.9 fusion.35
  46.1 1.3 collective-permute-done.2
  47.4 3.2 %collective-permute-done.3 = bf16[8,128,22,3]{1,3,2,0:T(4,128)(2,1)S(1)} collective-permute-done((bf16[8,128,22,3]{1,3,2,0:T(4,128)(2,1)S(1)}, bf16[8,128,22,3]{1,3,2,0:T(4,128)(2,1)S(1)}, u32[]{:S(2)}, u32[]{:S(2)}) %collective-permute-start.3) | collective-permute-done | bytes 135200 | tf_op jit(solution)/shard_map/ppermute | solution.py:22
  50.5 5.0 %maximum_multiply_fusion = bf16[8,128,22,134]{1,3,2,0:T(8,128)(2,1)} fusion(bf16[8,128,22,3]{1,3,2,0:T(4,128)(2,1)S(1)} %collective-permute-done.3, bf16[8,128,3,128]{1,3,2,0:T(8,128)(2,1)S(1)} %collective-permute-done.1, bf16[8,128,16,128]{1,3,2,0:T(8,128)(2,1)S(1)} %copy-done, bf16[8,128,3,128]{1,3,2,0:T(8,128)(2,1)S(1)} %collective-permute-done, ...), kind=kLoop, calls=%fused_computation.56 | loop fusion | flops 36225024 | bytes 12075276 | tf_op jit(solution)/shard_map/mul | solution.py:93
  55.5 72.9 %while.12 = (s32[]{:T(128)}, f32[8,12,18,130]{3,2,0,1:T(8,128)}, bf16[8,128,22,134]{1,3,2,0:T(8,128)(2,1)}, bf16[3,3,128,128]{3,2,1,0:T(8,128)(2,1)S(1)}, f32[12...) while((s32[]{:T(128)}, f32[8,12,18,130]{3,2,0,1:T(8,128)}, ...), condition=%wide.region_1.2_spmd.clone.clone, body=%wide.region_0.1_spmd.clone.clone.sunk | while | flops 845687296 | bytes 38270008 | solution.py:101
  55.5 1.2 dynamic-slice_bitcast_fusion.2
  58.4 2.1 %fusion.137 = bf16[128,20,132]{0,2,1:T(8,128)(2,1)S(1)} fusion(bf16[9,128,20,132]{1,3,0,2:T(8,128)(2,1)S(1)} %fusion.135, bf16[9,128,128,1]{2,1,0,3:T(8,128)(2,1)S(1)} %bitcast.198, f32[128]{0:T(128)S(1)} %get-tuple-element.213, bf16[132]{0:T(256)(128)(2,1)S(1)} %fusion.136), kind=kOutput, calls=%fused_computation.9.clone.1 | convolution fusion | flops 780933120 | bytes 7054088 | tf_op jit(solution)/shard_map/while/body/eval_jaxpr/tcxy,tco->oxy/dot_general | solution.py:76
  62.0 1.8 fusion.147
  63.8 0.9 copy_dynamic-update-slice_fusion.2
  64.7 1.2 dynamic-slice_bitcast_fusion.2
  67.5 2.1 %fusion.137 = bf16[128,20,132]{0,2,1:T(8,128)(2,1)S(1)} fusion(bf16[9,128,20,132]{1,3,0,2:T(8,128)(2,1)S(1)} %fusion.135, bf16[9,128,128,1]{2,1,0,3:T(8,128)(2,1)S(1)} %bitcast.198, f32[128]{0:T(128)S(1)} %get-tuple-element.213, bf16[132]{0:T(256)(128)(2,1)S(1)} %fusion.136), kind=kOutput, calls=%fused_computation.9.clone.1 | convolution fusion | flops 780933120 | bytes 7054088 | tf_op jit(solution)/shard_map/while/body/eval_jaxpr/tcxy,tco->oxy/dot_general | solution.py:76
  71.1 1.8 fusion.147
  72.9 0.9 copy_dynamic-update-slice_fusion.2
  73.8 1.2 dynamic-slice_bitcast_fusion.2
  76.6 2.1 %fusion.137 = bf16[128,20,132]{0,2,1:T(8,128)(2,1)S(1)} fusion(bf16[9,128,20,132]{1,3,0,2:T(8,128)(2,1)S(1)} %fusion.135, bf16[9,128,128,1]{2,1,0,3:T(8,128)(2,1)S(1)} %bitcast.198, f32[128]{0:T(128)S(1)} %get-tuple-element.213, bf16[132]{0:T(256)(128)(2,1)S(1)} %fusion.136), kind=kOutput, calls=%fused_computation.9.clone.1 | convolution fusion | flops 780933120 | bytes 7054088 | tf_op jit(solution)/shard_map/while/body/eval_jaxpr/tcxy,tco->oxy/dot_general | solution.py:76
  80.2 1.8 fusion.147
  82.0 0.9 copy_dynamic-update-slice_fusion.2
  82.9 1.2 dynamic-slice_bitcast_fusion.2
  85.7 2.1 %fusion.137 = bf16[128,20,132]{0,2,1:T(8,128)(2,1)S(1)} fusion(bf16[9,128,20,132]{1,3,0,2:T(8,128)(2,1)S(1)} %fusion.135, bf16[9,128,128,1]{2,1,0,3:T(8,128)(2,1)S(1)} %bitcast.198, f32[128]{0:T(128)S(1)} %get-tuple-element.213, bf16[132]{0:T(256)(128)(2,1)S(1)} %fusion.136), kind=kOutput, calls=%fused_computation.9.clone.1 | convolution fusion | flops 780933120 | bytes 7054088 | tf_op jit(solution)/shard_map/while/body/eval_jaxpr/tcxy,tco->oxy/dot_general | solution.py:76
  89.3 1.8 fusion.147
  91.1 0.9 copy_dynamic-update-slice_fusion.2
  92.0 1.2 dynamic-slice_bitcast_fusion.2
  94.8 2.1 %fusion.137 = bf16[128,20,132]{0,2,1:T(8,128)(2,1)S(1)} fusion(bf16[9,128,20,132]{1,3,0,2:T(8,128)(2,1)S(1)} %fusion.135, bf16[9,128,128,1]{2,1,0,3:T(8,128)(2,1)S(1)} %bitcast.198, f32[128]{0:T(128)S(1)} %get-tuple-element.213, bf16[132]{0:T(256)(128)(2,1)S(1)} %fusion.136), kind=kOutput, calls=%fused_computation.9.clone.1 | convolution fusion | flops 780933120 | bytes 7054088 | tf_op jit(solution)/shard_map/while/body/eval_jaxpr/tcxy,tco->oxy/dot_general | solution.py:76
  98.4 1.8 fusion.147
  100.2 0.9 copy_dynamic-update-slice_fusion.2
  101.1 1.2 dynamic-slice_bitcast_fusion.2
  103.9 2.1 %fusion.137 = bf16[128,20,132]{0,2,1:T(8,128)(2,1)S(1)} fusion(bf16[9,128,20,132]{1,3,0,2:T(8,128)(2,1)S(1)} %fusion.135, bf16[9,128,128,1]{2,1,0,3:T(8,128)(2,1)S(1)} %bitcast.198, f32[128]{0:T(128)S(1)} %get-tuple-element.213, bf16[132]{0:T(256)(128)(2,1)S(1)} %fusion.136), kind=kOutput, calls=%fused_computation.9.clone.1 | convolution fusion | flops 780933120 | bytes 7054088 | tf_op jit(solution)/shard_map/while/body/eval_jaxpr/tcxy,tco->oxy/dot_general | solution.py:76
  107.5 1.8 fusion.147
  109.3 0.9 copy_dynamic-update-slice_fusion.2
  110.2 1.2 dynamic-slice_bitcast_fusion.2
  113.0 2.1 %fusion.137 = bf16[128,20,132]{0,2,1:T(8,128)(2,1)S(1)} fusion(bf16[9,128,20,132]{1,3,0,2:T(8,128)(2,1)S(1)} %fusion.135, bf16[9,128,128,1]{2,1,0,3:T(8,128)(2,1)S(1)} %bitcast.198, f32[128]{0:T(128)S(1)} %get-tuple-element.213, bf16[132]{0:T(256)(128)(2,1)S(1)} %fusion.136), kind=kOutput, calls=%fused_computation.9.clone.1 | convolution fusion | flops 780933120 | bytes 7054088 | tf_op jit(solution)/shard_map/while/body/eval_jaxpr/tcxy,tco->oxy/dot_general | solution.py:76
  116.6 1.8 fusion.147
  118.4 0.9 copy_dynamic-update-slice_fusion.2
  119.3 1.2 dynamic-slice_bitcast_fusion.2
  122.1 2.1 %fusion.137 = bf16[128,20,132]{0,2,1:T(8,128)(2,1)S(1)} fusion(bf16[9,128,20,132]{1,3,0,2:T(8,128)(2,1)S(1)} %fusion.135, bf16[9,128,128,1]{2,1,0,3:T(8,128)(2,1)S(1)} %bitcast.198, f32[128]{0:T(128)S(1)} %get-tuple-element.213, bf16[132]{0:T(256)(128)(2,1)S(1)} %fusion.136), kind=kOutput, calls=%fused_computation.9.clone.1 | convolution fusion | flops 780933120 | bytes 7054088 | tf_op jit(solution)/shard_map/while/body/eval_jaxpr/tcxy,tco->oxy/dot_general | solution.py:76
  125.8 1.8 fusion.147
  127.6 0.9 copy_dynamic-update-slice_fusion.2
  128.4 2.0 %broadcast_multiply_fusion = (f32[6,8,18,130]{3,2,1,0:T(8,128)S(1)}, f32[6,8,18,130]{3,2,1,0:T(8,128)S(1)}, f32[6,8,18,130]{3,2,1,0:T(8,128)S(1)}) fusion(f32[130]{0:T(256)S(1)} %cosine_maximum_fusion, f32[12,8,18,130]{3,2,1,0:T(8,128)} %bitcast), kind=kLoop, calls=%fused_computation.71 | loop fusion | flops 112320 | bytes 2246920 | tf_op jit(solution)/shard_map/mul | solution.py:106
  130.4 1.1 multiply_add_fusion.2
  131.5 3.0 %collective-permute-start.10 = (f32[6,8,1,128]{3,2,1,0:T(1,128)S(1)}, f32[6,8,1,128]{3,2,1,0:T(1,128)S(1)}, u32[]{:S(2)}, u32[]{:S(2)}) collective-permute-start(f32[6,8,1,128]{3,2,1,0:T(1,128)S(1)} %get-tuple-element.133), channel_id=1, source_target_pairs={{4,0},{8,4},{12,8},{16,12},{20,16},{24,20},{28,24},{32,28},{36,32}... | collective-permute-start | bytes 73736 | tf_op jit(solution)/shard_map/ppermute | solution.py:36
  134.8 3.2 %collective-permute-start.8 = (f32[6,8,16,1]{3,2,1,0:T(8,128)S(1)}, f32[6,8,16,1]{3,2,1,0:T(8,128)S(1)}, u32[]{:S(2)}, u32[]{:S(2)}) collective-permute-start(f32[6,8,16,1]{3,2,1,0:T(8,128)S(1)} %get-tuple-element.134), channel_id=1, source_target_pairs={{0,1},{1,2},{2,3},{3,0},{4,5},{5,6},{6,7},{7,4},{8,9},{9,10},{10,1... | collective-permute-start | bytes 9224 | tf_op jit(solution)/shard_map/ppermute | solution.py:35
  138.1 8.3 %collective-permute-done.11 = f32[6,8,16,1]{3,2,1,0:T(8,128)S(1)} collective-permute-done((f32[6,8,16,1]{3,2,1,0:T(8,128)S(1)}, f32[6,8,16,1]{3,2,1,0:T(8,128)S(1)}, u32[]{:S(2)}, u32[]{:S(2)}) %collective-permute-start.11) | collective-permute-done | bytes 3104 | tf_op jit(solution)/shard_map/ppermute | solution.py:36
  146.4 0.7 fusion.34
  147.1 0.8 multiply_add_fusion.1
  148.0 6.4 %collective-permute-start.14 = (f32[6,8,1,128]{3,2,1,0:T(1,128)S(1)}, f32[6,8,1,128]{3,2,1,0:T(1,128)S(1)}, u32[]{:S(2)}, u32[]{:S(2)}) collective-permute-start(f32[6,8,1,128]{3,2,1,0:T(1,128)S(1)} %get-tuple-element.129), channel_id=1, source_target_pairs={{4,0},{8,4},{12,8},{16,12},{20,16},{24,20},{28,24},{32,28},{36,32}... | collective-permute-start | bytes 73736 | tf_op jit(solution)/shard_map/ppermute | solution.py:36
  154.6 3.8 %collective-permute-start.12 = (f32[6,8,16,1]{3,2,1,0:T(8,128)S(1)}, f32[6,8,16,1]{3,2,1,0:T(8,128)S(1)}, u32[]{:S(2)}, u32[]{:S(2)}) collective-permute-start(f32[6,8,16,1]{3,2,1,0:T(8,128)S(1)} %get-tuple-element.130), channel_id=1, source_target_pairs={{0,1},{1,2},{2,3},{3,0},{4,5},{5,6},{6,7},{7,4},{8,9},{9,10},{10,1... | collective-permute-start | bytes 9224 | tf_op jit(solution)/shard_map/ppermute | solution.py:35
  158.4 7.3 %collective-permute-done.12 = f32[6,8,16,1]{3,2,1,0:T(8,128)S(1)} collective-permute-done((f32[6,8,16,1]{3,2,1,0:T(8,128)S(1)}, f32[6,8,16,1]{3,2,1,0:T(8,128)S(1)}, u32[]{:S(2)}, u32[]{:S(2)}) %collective-permute-start.12) | collective-permute-done | bytes 3104 | tf_op jit(solution)/shard_map/ppermute | solution.py:35
  165.8 3.0 %collective-permute-done.15 = f32[6,8,16,1]{3,2,1,0:T(8,128)S(1)} collective-permute-done((f32[6,8,16,1]{3,2,1,0:T(8,128)S(1)}, f32[6,8,16,1]{3,2,1,0:T(8,128)S(1)}, u32[]{:S(2)}, u32[]{:S(2)}) %collective-permute-start.15) | collective-permute-done | bytes 3104 | tf_op jit(solution)/shard_map/ppermute | solution.py:36
  169.6 0.8 multiply_add_fusion
  170.5 5.7 %collective-permute-start.18 = (f32[6,8,1,128]{3,2,1,0:T(1,128)S(1)}, f32[6,8,1,128]{3,2,1,0:T(1,128)S(1)}, u32[]{:S(2)}, u32[]{:S(2)}) collective-permute-start(f32[6,8,1,128]{3,2,1,0:T(1,128)S(1)} %get-tuple-element.125), channel_id=1, source_target_pairs={{4,0},{8,4},{12,8},{16,12},{20,16},{24,20},{28,24},{32,28},{36,32}... | collective-permute-start | bytes 73736 | tf_op jit(solution)/shard_map/ppermute | solution.py:36
  176.3 1.6 collective-permute-start.16
  177.9 2.8 %slice.306 = f32[12,8,16,128]{3,2,1,0:T(8,128)} slice(f32[12,8,18,130]{3,2,1,0:T(8,128)} %bitcast), slice={[0:12], [0:8], [1:17], [1:129]} | slice | bytes 1572864 | tf_op jit(solution)/shard_map/slice | solution.py:51
  180.7 4.7 %collective-permute-done.16 = f32[6,8,16,1]{3,2,1,0:T(8,128)S(1)} collective-permute-done((f32[6,8,16,1]{3,2,1,0:T(8,128)S(1)}, f32[6,8,16,1]{3,2,1,0:T(8,128)S(1)}, u32[]{:S(2)}, u32[]{:S(2)}) %collective-permute-start.16) | collective-permute-done | bytes 3104 | tf_op jit(solution)/shard_map/ppermute | solution.py:35
  185.4 2.7 %collective-permute-done.19 = f32[6,8,16,1]{3,2,1,0:T(8,128)S(1)} collective-permute-done((f32[6,8,16,1]{3,2,1,0:T(8,128)S(1)}, f32[6,8,16,1]{3,2,1,0:T(8,128)S(1)}, u32[]{:S(2)}, u32[]{:S(2)}) %collective-permute-start.19) | collective-permute-done | bytes 3104 | tf_op jit(solution)/shard_map/ppermute | solution.py:36
  188.9 1.5 fusion.41
  (208 shorter events, 27.8 us)
Async XLA Ops:
  7.4 12.2 %copy-start.1 = (f32[6,8,16,128]{3,2,1,0:T(8,128)S(1)}, f32[6,8,16,128]{3,2,1,0:T(8,128)}, u32[]{:S(2)}) copy-start(f32[6,8,16,128]{3,2,1,0:T(8,128)} %param.13) | copy-start | bytes 1179652
  9.8 27.3 %collective-permute-start = (bf16[8,128,3,128]{1,3,2,0:T(8,128)(2,1)}, bf16[8,128,3,128]{1,3,2,0:T(8,128)(2,1)S(1)}, u32[]{:S(2)}, u32[]{:S(2)}) collective-permute-start(bf16[8,128,3,128]{1,3,2,0:T(8,128)(2,1)} %get-tuple-element.119), channel_id=1, source_target_pairs={{0,4},{4,8},{8,12},{12,16},{16,20},{20,24},{24,28},{28,32},{32,36}... | collective-permute-start | bytes 2359304 | tf_op jit(solution)/shard_map/ppermute | solution.py:19
  12.3 26.0 %collective-permute-start.1 = (bf16[8,128,3,128]{1,3,2,0:T(8,128)(2,1)S(1)}, bf16[8,128,3,128]{1,3,2,0:T(8,128)(2,1)S(1)}, u32[]{:S(2)}, u32[]{:S(2)}) collective-permute-start(bf16[8,128,3,128]{1,3,2,0:T(8,128)(2,1)S(1)} %get-tuple-element.120), channel_id=1, source_target_pairs={{4,0},{8,4},{12,8},{16,12},{20,16},{24,20},{28,24},{32,28},{36,32}... | collective-permute-start | bytes 2359304 | tf_op jit(solution)/shard_map/ppermute | solution.py:22
  19.8 24.3 %collective-permute-start.4 = (f32[6,8,16,1]{3,2,1,0:T(8,128)S(1)}, f32[6,8,16,1]{3,2,1,0:T(8,128)}, u32[]{:S(2)}, u32[]{:S(2)}) collective-permute-start(f32[6,8,16,1]{3,2,1,0:T(8,128)S(1)} %get-tuple-element.138), channel_id=1, source_target_pairs={{0,1},{1,2},{2,3},{3,0},{4,5},{5,6},{6,7},{7,4},{8,9},{9,10},{10,1... | collective-permute-start | bytes 9224 | tf_op jit(solution)/shard_map/ppermute | solution.py:35
  23.2 20.9 %collective-permute-start.7 = (f32[6,8,16,1]{3,2,1,0:T(8,128)S(1)}, f32[6,8,16,1]{3,2,1,0:T(8,128)}, u32[]{:S(2)}, u32[]{:S(2)}) collective-permute-start(f32[6,8,16,1]{3,2,1,0:T(8,128)S(1)} %get-tuple-element.139), channel_id=1, source_target_pairs={{1,0},{2,1},{3,2},{0,3},{5,4},{6,5},{7,6},{4,7},{9,8},{10,9},{11,1... | collective-permute-start | bytes 9224 | tf_op jit(solution)/shard_map/ppermute | solution.py:36
  23.8 20.3 %collective-permute-start.5 = (f32[6,8,1,128]{3,2,1,0:T(1,128)}, f32[6,8,1,128]{3,2,1,0:T(1,128)}, u32[]{:S(2)}, u32[]{:S(2)}) collective-permute-start(f32[6,8,1,128]{3,2,1,0:T(1,128)} %get-tuple-element.136), channel_id=1, source_target_pairs={{0,4},{4,8},{8,12},{12,16},{16,20},{20,24},{24,28},{28,32},{32,36}... | collective-permute-start | bytes 73736 | tf_op jit(solution)/shard_map/ppermute | solution.py:35
  37.1 7.0 %collective-permute-start.6 = (f32[6,8,1,128]{3,2,1,0:T(1,128)}, f32[6,8,1,128]{3,2,1,0:T(1,128)S(1)}, u32[]{:S(2)}, u32[]{:S(2)}) collective-permute-start(f32[6,8,1,128]{3,2,1,0:T(1,128)} %get-tuple-element.137), channel_id=1, source_target_pairs={{4,0},{8,4},{12,8},{16,12},{20,16},{24,20},{28,24},{32,28},{36,32}... | collective-permute-start | bytes 73736 | tf_op jit(solution)/shard_map/ppermute | solution.py:36
  38.3 12.3 %copy-start = (bf16[8,128,16,128]{1,3,2,0:T(8,128)(2,1)S(1)}, bf16[8,128,16,128]{1,3,2,0:T(8,128)(2,1)}, u32[]{:S(2)}) copy-start(bf16[8,128,16,128]{1,3,2,0:T(8,128)(2,1)} %copy.17) | copy-start | bytes 12582916
  39.6 7.8 %collective-permute-start.2 = (bf16[8,128,22,3]{1,3,2,0:T(4,128)(2,1)S(1)}, bf16[8,128,22,3]{1,3,2,0:T(4,128)(2,1)S(1)}, u32[]{:S(2)}, u32[]{:S(2)}) collective-permute-start(bf16[8,128,22,3]{1,3,2,0:T(4,128)(2,1)S(1)} %get-tuple-element.117), channel_id=1, source_target_pairs={{0,1},{1,2},{2,3},{3,0},{4,5},{5,6},{6,7},{7,4},{8,9},{9,10},{10,1... | collective-permute-start | bytes 405512 | tf_op jit(solution)/shard_map/ppermute | solution.py:19
  44.1 6.4 %collective-permute-start.3 = (bf16[8,128,22,3]{1,3,2,0:T(4,128)(2,1)S(1)}, bf16[8,128,22,3]{1,3,2,0:T(4,128)(2,1)S(1)}, u32[]{:S(2)}, u32[]{:S(2)}) collective-permute-start(bf16[8,128,22,3]{1,3,2,0:T(4,128)(2,1)S(1)} %get-tuple-element.118), channel_id=1, source_target_pairs={{1,0},{2,1},{3,2},{0,3},{5,4},{6,5},{7,6},{4,7},{9,8},{10,9},{11,1... | collective-permute-start | bytes 405512 | tf_op jit(solution)/shard_map/ppermute | solution.py:22
  46.0 9.5 %copy-start.2 = (bf16[3,3,128,12]{2,3,1,0:T(8,128)(2,1)S(1)}, bf16[3,3,128,12]{2,3,1,0:T(8,128)(2,1)}, u32[]{:S(2)}) copy-start(bf16[3,3,128,12]{2,3,1,0:T(8,128)(2,1)} %param.11) | copy-start | bytes 82948
  46.0 9.5 %copy-start.3 = (f32[12]{0:T(128)S(1)}, f32[12]{0:T(128)}, u32[]{:S(2)}) copy-start(f32[12]{0:T(128)} %param.12) | copy-start | bytes 148
  46.0 9.5 %copy-start.4 = (bf16[3,3,128,128]{3,2,1,0:T(8,128)(2,1)S(1)}, bf16[3,3,128,128]{3,2,1,0:T(8,128)(2,1)}, u32[]{:S(2)}) copy-start(bf16[3,3,128,128]{3,2,1,0:T(8,128)(2,1)} %param.9) | copy-start | bytes 884740
  46.0 9.5 %copy-start.5 = (f32[128]{0:T(128)S(1)}, f32[128]{0:T(128)}, u32[]{:S(2)}) copy-start(f32[128]{0:T(128)} %param.10) | copy-start | bytes 1540
  131.5 14.8 %collective-permute-start.10 = (f32[6,8,1,128]{3,2,1,0:T(1,128)S(1)}, f32[6,8,1,128]{3,2,1,0:T(1,128)S(1)}, u32[]{:S(2)}, u32[]{:S(2)}) collective-permute-start(f32[6,8,1,128]{3,2,1,0:T(1,128)S(1)} %get-tuple-element.133), channel_id=1, source_target_pairs={{4,0},{8,4},{12,8},{16,12},{20,16},{24,20},{28,24},{32,28},{36,32}... | collective-permute-start | bytes 73736 | tf_op jit(solution)/shard_map/ppermute | solution.py:36
  134.5 11.8 %collective-permute-start.9 = (f32[6,8,1,128]{3,2,1,0:T(1,128)S(1)}, f32[6,8,1,128]{3,2,1,0:T(1,128)S(1)}, u32[]{:S(2)}, u32[]{:S(2)}) collective-permute-start(f32[6,8,1,128]{3,2,1,0:T(1,128)S(1)} %get-tuple-element.132), channel_id=1, source_target_pairs={{0,4},{4,8},{8,12},{12,16},{16,20},{20,24},{24,28},{28,32},{32,36}... | collective-permute-start | bytes 73736 | tf_op jit(solution)/shard_map/ppermute | solution.py:35
  134.7 11.6 %collective-permute-start.11 = (f32[6,8,16,1]{3,2,1,0:T(8,128)S(1)}, f32[6,8,16,1]{3,2,1,0:T(8,128)S(1)}, u32[]{:S(2)}, u32[]{:S(2)}) collective-permute-start(f32[6,8,16,1]{3,2,1,0:T(8,128)S(1)} %get-tuple-element.135), channel_id=1, source_target_pairs={{1,0},{2,1},{3,2},{0,3},{5,4},{6,5},{7,6},{4,7},{9,8},{10,9},{11,1... | collective-permute-start | bytes 9224 | tf_op jit(solution)/shard_map/ppermute | solution.py:36
  134.8 11.5 %collective-permute-start.8 = (f32[6,8,16,1]{3,2,1,0:T(8,128)S(1)}, f32[6,8,16,1]{3,2,1,0:T(8,128)S(1)}, u32[]{:S(2)}, u32[]{:S(2)}) collective-permute-start(f32[6,8,16,1]{3,2,1,0:T(8,128)S(1)} %get-tuple-element.134), channel_id=1, source_target_pairs={{0,1},{1,2},{2,3},{3,0},{4,5},{5,6},{6,7},{7,4},{8,9},{9,10},{10,1... | collective-permute-start | bytes 9224 | tf_op jit(solution)/shard_map/ppermute | solution.py:35
  147.9 20.9 %collective-permute-start.13 = (f32[6,8,1,128]{3,2,1,0:T(1,128)S(1)}, f32[6,8,1,128]{3,2,1,0:T(1,128)S(1)}, u32[]{:S(2)}, u32[]{:S(2)}) collective-permute-start(f32[6,8,1,128]{3,2,1,0:T(1,128)S(1)} %get-tuple-element.128), channel_id=1, source_target_pairs={{0,4},{4,8},{8,12},{12,16},{16,20},{20,24},{24,28},{28,32},{32,36}... | collective-permute-start | bytes 73736 | tf_op jit(solution)/shard_map/ppermute | solution.py:35
  148.0 20.8 %collective-permute-start.14 = (f32[6,8,1,128]{3,2,1,0:T(1,128)S(1)}, f32[6,8,1,128]{3,2,1,0:T(1,128)S(1)}, u32[]{:S(2)}, u32[]{:S(2)}) collective-permute-start(f32[6,8,1,128]{3,2,1,0:T(1,128)S(1)} %get-tuple-element.129), channel_id=1, source_target_pairs={{4,0},{8,4},{12,8},{16,12},{20,16},{24,20},{28,24},{32,28},{36,32}... | collective-permute-start | bytes 73736 | tf_op jit(solution)/shard_map/ppermute | solution.py:36
  154.6 11.2 %collective-permute-start.12 = (f32[6,8,16,1]{3,2,1,0:T(8,128)S(1)}, f32[6,8,16,1]{3,2,1,0:T(8,128)S(1)}, u32[]{:S(2)}, u32[]{:S(2)}) collective-permute-start(f32[6,8,16,1]{3,2,1,0:T(8,128)S(1)} %get-tuple-element.130), channel_id=1, source_target_pairs={{0,1},{1,2},{2,3},{3,0},{4,5},{5,6},{6,7},{7,4},{8,9},{9,10},{10,1... | collective-permute-start | bytes 9224 | tf_op jit(solution)/shard_map/ppermute | solution.py:35
  158.4 10.4 %collective-permute-start.15 = (f32[6,8,16,1]{3,2,1,0:T(8,128)S(1)}, f32[6,8,16,1]{3,2,1,0:T(8,128)S(1)}, u32[]{:S(2)}, u32[]{:S(2)}) collective-permute-start(f32[6,8,16,1]{3,2,1,0:T(8,128)S(1)} %get-tuple-element.131), channel_id=1, source_target_pairs={{1,0},{2,1},{3,2},{0,3},{5,4},{6,5},{7,6},{4,7},{9,8},{10,9},{11,1... | collective-permute-start | bytes 9224 | tf_op jit(solution)/shard_map/ppermute | solution.py:36
  170.4 17.8 %collective-permute-start.17 = (f32[6,8,1,128]{3,2,1,0:T(1,128)S(1)}, f32[6,8,1,128]{3,2,1,0:T(1,128)S(1)}, u32[]{:S(2)}, u32[]{:S(2)}) collective-permute-start(f32[6,8,1,128]{3,2,1,0:T(1,128)S(1)} %get-tuple-element.124), channel_id=1, source_target_pairs={{0,4},{4,8},{8,12},{12,16},{16,20},{20,24},{24,28},{28,32},{32,36}... | collective-permute-start | bytes 73736 | tf_op jit(solution)/shard_map/ppermute | solution.py:35
  170.5 17.7 %collective-permute-start.18 = (f32[6,8,1,128]{3,2,1,0:T(1,128)S(1)}, f32[6,8,1,128]{3,2,1,0:T(1,128)S(1)}, u32[]{:S(2)}, u32[]{:S(2)}) collective-permute-start(f32[6,8,1,128]{3,2,1,0:T(1,128)S(1)} %get-tuple-element.125), channel_id=1, source_target_pairs={{4,0},{8,4},{12,8},{16,12},{20,16},{24,20},{28,24},{32,28},{36,32}... | collective-permute-start | bytes 73736 | tf_op jit(solution)/shard_map/ppermute | solution.py:36
  176.3 9.1 %collective-permute-start.16 = (f32[6,8,16,1]{3,2,1,0:T(8,128)S(1)}, f32[6,8,16,1]{3,2,1,0:T(8,128)S(1)}, u32[]{:S(2)}, u32[]{:S(2)}) collective-permute-start(f32[6,8,16,1]{3,2,1,0:T(8,128)S(1)} %get-tuple-element.126), channel_id=1, source_target_pairs={{0,1},{1,2},{2,3},{3,0},{4,5},{5,6},{6,7},{7,4},{8,9},{9,10},{10,1... | collective-permute-start | bytes 9224 | tf_op jit(solution)/shard_map/ppermute | solution.py:35
  177.9 10.2 %collective-permute-start.19 = (f32[6,8,16,1]{3,2,1,0:T(8,128)S(1)}, f32[6,8,16,1]{3,2,1,0:T(8,128)S(1)}, u32[]{:S(2)}, u32[]{:S(2)}) collective-permute-start(f32[6,8,16,1]{3,2,1,0:T(8,128)S(1)} %get-tuple-element.127), channel_id=1, source_target_pairs={{1,0},{2,1},{3,2},{0,3},{5,4},{6,5},{7,6},{4,7},{9,8},{10,9},{11,1... | collective-permute-start | bytes 9224 | tf_op jit(solution)/shard_map/ppermute | solution.py:36
where the time goes:
time: 191 us; the launch traced here: 190 us
  local copies, waits for them, and re-layouts  54.3 us (28%)
  waiting for transfers between devices  43.8 us (23%)
  starting transfers between devices  42.8 us (22%)
  matrix products  31.1 us (16%)
  other arithmetic  16.7 us (9%)
    dot_general x16, matrix products, conv_block(): jnp.einsum('tcxy,tco->oxy', taps, stacked, preferred_element_type=jnp.flo...  31.1 us
    while x128, local copies, waits for them, and re-layouts  20.9 us
    ppermute x8, starting transfers between devices, with_halo(): lax.ppermute(leading, axis, [(b, a) for a, b in up])  16.3 us
    ppermute x2, waiting for transfers between devices, padded_2(): lax.ppermute(lax.slice_in_dim(block, block.shape[dim] - width, None, axis...  14.5 us
    ppermute x8, waiting for transfers between devices, with_halo(): lax.ppermute(leading, axis, [(b, a) for a, b in up])  14.1 us
    ppermute x8, starting transfers between devices, with_halo(): lax.ppermute(last, axis, up)  12.2 us
    ppermute x8, waiting for transfers between devices, with_halo(): lax.ppermute(last, axis, up)  12 us
    squeeze x8, local copies, waits for them, and re-layouts, body(): wide = jnp.transpose(lax.map(level, padded), (1, 0, 2, 3))  9.44 us
  transfers between devices with their start and end apart: 20, of which 8 were waited for; matrix products, arithmetic and copies ran while one was open for 4% of the time, Pallas kernels for 0%

commit v1 on v0

v1 whole, which is shorter than its diff:
```python
import functools
import math

import jax
import jax.numpy as jnp
import numpy as np
from jax import lax
from jax.experimental import pallas as pl
from jax.experimental.pallas import tpu as pltpu
from jax.sharding import PartitionSpec as P

MESH = pl.DeviceIdType.MESH
F32 = jnp.float32
BF16 = jnp.bfloat16
TIME_STEP = 0.5
SPEED_CAP = 0.6
COS_FLOOR = 0.5
NV = 6
NC = 12
NF = 18
LV = 8
NX = 16
NY = 128
CH = 128
M = 4
EX = NX + 2 * M
NR = NX + 2


def lat_tables(n_lat_dev):
    n_lat = n_lat_dev * NY
    out = np.zeros((n_lat_dev, 2, LV, 2 * NY), np.float32)
    for d in range(n_lat_dev):
        lane = np.arange(2 * NY)
        y = np.where(lane < NY + NY // 2, lane, lane - 2 * NY) + d * NY
        phi = (y + 0.5) * (math.pi / n_lat) - 0.5 * math.pi
        inside = ((y >= 0) & (y < n_lat)).astype(np.float32)
        out[d, 0] = np.maximum(np.cos(phi), COS_FLOOR)[None]
        out[d, 1] = (SPEED_CAP * inside)[None]
    return out


def lanes(shape):
    return lax.broadcasted_iota(jnp.int32, shape, len(shape) - 1)


def roll(v, s):
    s = s % NY
    return v if s == 0 else pltpu.roll(v, s, v.ndim - 1)


def kernel(n_lon, n_lat, x_hbm, w1_ref, b1_ref, w2_ref, b2_ref, st_ref, tab_ref,
           vel_ref, tend_ref,
           xin, xt, ht, lhs1, lhs2, oh, ohe, bias, xe, xh, xc, pm, pe, fm, fe, pk, pr, rowr, epk, epr,
           in_sem, ls, lr, ns, nr, ps, prs, rs, rr, qls, qlr, qs, qr):
    lon = lax.axis_index("lon")
    lat = lax.axis_index("lat")
    left = (lax.rem(lon + n_lon - 1, n_lon), lat)
    right = (lax.rem(lon + 1, n_lon), lat)
    south = (lon, lat - 1)
    north = (lon, lat + 1)
    has_s = lat > 0
    has_n = lat < n_lat - 1

    xh[...] = jnp.zeros_like(xh)
    pr[...] = jnp.zeros_like(pr)

    barrier = pltpu.get_barrier_semaphore()
    for dev in (left, right):
        pl.semaphore_signal(barrier, inc=1, device_id=dev, device_id_type=MESH)

    @pl.when(has_s)
    def _():
        pl.semaphore_signal(barrier, inc=1, device_id=south, device_id_type=MESH)

    @pl.when(has_n)
    def _():
        pl.semaphore_signal(barrier, inc=1, device_id=north, device_id_type=MESH)

    loads = [pltpu.make_async_copy(x_hbm.at[l], xin.at[l], in_sem.at[l]) for l in range(LV)]
    for c in loads:
        c.start()

    for b in range(3):
        for a in range(3):
            lhs1[0, b * CH:(b + 1) * CH, a * CH:(a + 1) * CH] = jnp.transpose(w1_ref[a, b], (1, 0))
    for lp in range(1, LV // 2):
        lhs1[lp, :, 0:3 * CH] = lhs1[0, :, 0:3 * CH]
    lhs2[...] = jnp.zeros_like(lhs2)
    for b in range(3):
        for off in range(4):
            for r in range(2):
                a = r - off + 2
                if 0 <= a <= 2:
                    base = b * 64 + off * 16
                    lhs2[base:base + NC, r * CH:(r + 1) * CH] = w2_ref[a, b]
    bias[...] = jnp.transpose(jnp.broadcast_to(b1_ref[...], (CH, CH)), (1, 0))
    k_id = lax.broadcasted_iota(jnp.int32, (CH, 2 * NY), 0)
    lane2 = lanes((CH, 2 * NY))
    half = (k_id // 16) % 2
    target = half * NY + jnp.where(k_id < 64, 0, NY - 1)
    hit = lane2 == target

    @pl.loop(0, NX)
    def _(x):
        oh[x] = jnp.where(hit & (k_id % 16 == x), 1.0, 0.0).astype(BF16)
        want_hi = (k_id == NY - 1) & (lane2 == x)
        want_lo = (k_id == 0) & (lane2 == NY + x)
        ohe[x] = jnp.where(want_hi | want_lo, 1.0, 0.0).astype(BF16)

    zero_rows = jnp.zeros((NF, M, LV, NY), F32)
    fe[:, 0:M] = zero_rows
    fe[:, M + NX:EX] = zero_rows
    fm[0:NC, 0:M] = zero_rows[:NC]
    fm[0:NC, M + NX:EX] = zero_rows[:NC]
    for v in range(NV):
        fm[NC + v, M:M + NX] = jnp.transpose(st_ref[v], (1, 0, 2))

    hi = jnp.zeros((CH, NY), F32)
    lo = jnp.zeros((CH, NY), F32)
    for l in range(LV):
        loads[l].wait()
        xt[l, 1:NX + 1] = jnp.transpose(xin[l], (1, 0, 2))
        row = jnp.concatenate([xt[l, 1 + x] for x in range(NX)], axis=1)
        res = jnp.dot(row, ohe[...].reshape(NX * NY, 2 * NY), preferred_element_type=F32)
        hi = hi + roll(res[:, :NY], 16 * l)
        lo = lo + roll(res[:, NY:], 16 * l)
    xe[0] = hi.astype(BF16)
    xe[1] = lo.astype(BF16)

    pl.semaphore_wait(barrier, 2 + has_s.astype(jnp.int32) + has_n.astype(jnp.int32))

    def rcopy(src, dst, ss, rs_, dev):
        return pltpu.make_async_remote_copy(src_ref=src, dst_ref=dst, send_sem=ss, recv_sem=rs_,
                                            device_id=dev, device_id_type=MESH)

    def lat_exchange(src_n, src_s, dst_from_s, dst_from_n, sems, semr):
        to_n = rcopy(src_n, dst_from_s, sems.at[0], semr.at[0], north)
        to_s = rcopy(src_s, dst_from_n, sems.at[1], semr.at[1], south)

        @pl.when(has_n)
        def _():
            to_n.start()

        @pl.when(has_s)
        def _():
            to_s.start()

        def finish():
            @pl.when(has_s)
            def _():
                to_n.wait_recv()
                to_s.wait_send()

            @pl.when(has_n)
            def _():
                to_s.wait_recv()
                to_n.wait_send()
        return finish

    lane8 = lanes((LV, NY))

    def pack_lat(f, get_m, get_e):
        to_n = jnp.zeros((LV, NY), F32)
        to_s = jnp.zeros((LV, NY), F32)
        for r in range(NR):
            m = get_m(r)
            e = get_e(r)
            mine = (lane8 >= 5 * r) & (lane8 < 5 * r + 5)
            to_n = jnp.where(mine, roll(jnp.where(lane8 == 0, e, m), 5 * r + 4), to_n)
            to_s = jnp.where(mine, roll(jnp.where(lane8 == NY - 1, e, m), 5 * r + 1), to_s)
        pk[0, f] = to_n
        pk[1, f] = to_s

    def add_lat(f, get_m, get_e):
        edges = []
        for r in range(NR):
            a = roll(pr[0, f], -(5 * r + 4))
            b = roll(pr[1, f], -(5 * r + 1))
            if get_m is not None:
                fm[f, M - 1 + r] = get_m(r) + jnp.where(lane8 == 0, a, 0.0) + jnp.where(lane8 == NY - 1, b, 0.0)
            edge = get_e(r) + jnp.where(lane8 >= NY - 4, a, 0.0) + jnp.where(lane8 < 4, b, 0.0)
            fe[f, M - 1 + r] = edge
            edges.append(edge)
        for side in range(2):
            acc = jnp.zeros((LV, NY), F32)
            for r in range(5):
                src = edges[r if side == 0 else NR - 5 + r]
                acc = jnp.where((lane8 >= 8 * r) & (lane8 < 8 * r + 8), roll(src, 8 * r + 4), acc)
            epk[side, f] = acc

    def add_edge_rows(f):
        for side in range(2):
            for r in range(5):
                x = (r if side == 0 else M + NX - 1 + r)
                t = roll(epr[side, f], -(8 * r + 4))
                fe[f, x] = fe[f, x] + jnp.where((lane8 < 4) | (lane8 >= NY - 4), t, 0.0)

    x_lat = lat_exchange(xe.at[0], xe.at[1], xh.at[0], xh.at[1], ls, lr)
    x_left = rcopy(xt.at[:, 1], xt.at[:, NX + 1], ns.at[0], nr.at[0], left)
    x_right = rcopy(xt.at[:, NX], xt.at[:, 0], ns.at[1], nr.at[1], right)
    x_left.start()
    x_right.start()
    x_lat()
    c_left = rcopy(xh, xc.at[1], ns.at[2], nr.at[2], left)
    c_right = rcopy(xh, xc.at[0], ns.at[3], nr.at[3], right)
    c_left.start()
    c_right.start()
    c_left.wait()
    c_right.wait()

    xpos = lanes((CH, NY)) % NX
    kinds = []
    for side in range(2):
        b = 2 * side
        own = xh[side].astype(F32)
        from_l = xc[0, side].astype(F32)
        from_r = xc[1, side].astype(F32)
        t0 = jnp.where(xpos == 0, roll(from_l, -(NX - 1)), roll(own, 1)).astype(BF16)
        t2 = jnp.where(xpos == NX - 1, roll(from_r, NX - 1), roll(own, -1)).astype(BF16)
        taps = jnp.concatenate([t0, xh[side], t2], axis=0)
        e = jnp.dot(lhs1[0, b * CH:(b + 1) * CH, 0:3 * CH], taps, preferred_element_type=F32)
        e_hi = e.astype(BF16).astype(F32)
        kinds += [e_hi, e - e_hi]
    group = lanes((CH, NY)) // 32
    for lp in range(LV // 2):
        inj = jnp.zeros((CH, NY), F32)
        for kind in range(4):
            inj = jnp.where(group == kind, roll(kinds[kind], 32 * kind - 32 * lp), inj)
        zero = jnp.zeros((CH, NY), BF16)
        lhs1[lp, 0:CH, 3 * CH:] = zero
        lhs1[lp, CH:2 * CH, 3 * CH:] = inj.astype(BF16)
        lhs1[lp, 2 * CH:, 3 * CH:] = zero

    zero8 = jnp.zeros((LV, NY), F32)

    @pl.loop(NC, NF)
    def _(f):
        pack_lat(f, lambda r: fm[f, M - 1 + r] if 0 < r < NR - 1 else zero8, lambda r: zero8)

    q_left = rcopy(fm.at[NC:NF, M:M + 4], fm.at[NC:NF, M + NX:M + NX + 4], qs.at[0], qr.at[0], left)
    q_right = rcopy(fm.at[NC:NF, M + NX - 4:M + NX], fm.at[NC:NF, 0:4], qs.at[1], qr.at[1], right)
    q_left.start()
    q_right.start()
    q_lat = lat_exchange(pk.at[0, NC:NF], pk.at[1, NC:NF], pr.at[0, NC:NF], pr.at[1, NC:NF], qls, qlr)
    q_lat()

    @pl.loop(NC, NF)
    def _(f):
        add_lat(f, None, lambda r: zero8)

    qe_left = rcopy(epk.at[0, NC:NF], epr.at[1, NC:NF], qs.at[2], qr.at[2], left)
    qe_right = rcopy(epk.at[1, NC:NF], epr.at[0, NC:NF], qs.at[3], qr.at[3], right)
    qe_left.start()
    qe_right.start()
    q_copies = [q_left, q_right, qe_left, qe_right]

    x_left.wait()
    x_right.wait()

    lane1 = lanes((CH, NY))

    @pl.loop(0, LV // 2)
    def _(lp):
        @pl.loop(0, NX)
        def _(x):
            rhs = jnp.concatenate(
                [xt[2 * lp + h, pl.ds(x, 3)].reshape(3 * CH, NY) for h in range(2)], axis=1)
            rhs = jnp.concatenate([rhs, oh[x]], axis=0)
            s = jnp.dot(lhs1[lp], rhs, preferred_element_type=F32)
            for h in range(2):
                c = slice(h * NY, (h + 1) * NY)
                pre = s[CH:2 * CH, c] + bias[...]
                pre = pre + jnp.where(lane1 == 0, 0.0, roll(s[0:CH, c], 1))
                pre = pre + jnp.where(lane1 == NY - 1, 0.0, roll(s[2 * CH:, c], -1))
                half_pre = 0.5 * pre
                ht[2 * lp + h, x] = (half_pre + half_pre * jnp.tanh(half_pre)).astype(BF16)

    lane64 = lanes((64, NY))

    @pl.loop(0, LV // 2)
    def _(lp):
        prev = [None, None]
        for p in range(NX // 2):
            rhs = jnp.concatenate(
                [ht[2 * lp + h, 2 * p:2 * p + 2].reshape(2 * CH, NY) for h in range(2)], axis=1)
            s = jnp.dot(lhs2[...], rhs, preferred_element_type=F32)
            for h in range(2):
                c = slice(h * NY, (h + 1) * NY)
                up = roll(s[0:64, c], 1)
                dn = roll(s[128:192, c], -1)
                main = s[64:128, c] + jnp.where(lane64 == 0, 0.0, up) + jnp.where(lane64 == NY - 1, 0.0, dn)
                edge = jnp.where(lane64 == 0, up, 0.0) + jnp.where(lane64 == NY - 1, dn, 0.0)
                now = (main, edge)
                l = 2 * lp + h
                rows = [(2 * p - 1, 0), (2 * p, 1)]
                if p == NX // 2 - 1:
                    rows += [(2 * p + 1, 2), (2 * p + 2, 3)]
                for xo, off in rows:
                    for ref, val, old in zip((pm, pe), now, prev[h] or (None, None)):
                        t = val[off * 16:off * 16 + NC]
                        if off < 2 and old is not None:
                            t = t + old[(off + 2) * 16:(off + 2) * 16 + NC]
                        ref[pl.ds((xo + 1) * LV + l, NC, stride=NR * LV), :] = t
                prev[h] = now

    @pl.loop(0, NC)
    def _(f):
        pack_lat(f, lambda r: pm[pl.ds((f * NR + r) * LV, LV), :], lambda r: pe[pl.ds((f * NR + r) * LV, LV), :])

    lat_exchange(pk.at[0, 0:NC], pk.at[1, 0:NC], pr.at[0, 0:NC], pr.at[1, 0:NC], ps, prs)()

    @pl.loop(0, NC)
    def _(f):
        add_lat(f, lambda r: pm[pl.ds((f * NR + r) * LV, LV), :], lambda r: pe[pl.ds((f * NR + r) * LV, LV), :])

    r_left = rcopy(fm.at[0:NC, M - 1:M + 4], rowr.at[1], rs.at[0], rr.at[0], left)
    r_right = rcopy(fm.at[0:NC, M + NX - 4:M + NX + 1], rowr.at[0], rs.at[1], rr.at[1], right)
    e_left = rcopy(epk.at[0, 0:NC], epr.at[1, 0:NC], rs.at[2], rr.at[2], left)
    e_right = rcopy(epk.at[1, 0:NC], epr.at[0, 0:NC], rs.at[3], rr.at[3], right)
    for c in (e_left, e_right, r_left, r_right):
        c.start()
    for c in (e_left, e_right, r_left, r_right):
        c.wait()

    @pl.loop(0, NC)
    def _(f):
        for side in range(2):
            for r in range(5):
                x = (r if side == 0 else M + NX - 1 + r)
                fm[f, x] = fm[f, x] + rowr[side, f, r]
        add_edge_rows(f)

    for c in q_copies:
        c.wait()

    @pl.loop(NC, NF)
    def _(f):
        add_edge_rows(f)

    cos_m = tab_ref[lat, 0, :, 0:NY]
    cos_e = tab_ref[lat, 0, :, NY:]
    cap_m = tab_ref[lat, 1, :, 0:NY]
    cap_e = tab_ref[lat, 1, :, NY:]
    met_m = 1.0 / cos_m
    met_e = 1.0 / cos_e

    def shift(m, e, step):
        sh = 1 if step < 0 else -1
        edge = 0 if step < 0 else NY - 1
        rm, re = roll(m, sh), roll(e, sh)
        at = lanes(m.shape) == edge
        return jnp.where(at, re, rm), jnp.where(at, rm, re)

    @pl.loop(0, NV)
    def _(v):
        bu = b2_ref[2 * v]
        bv = b2_ref[2 * v + 1]
        um = cap_m * jnp.tanh(fm[2 * v] + bu)
        ue = cap_e * jnp.tanh(fe[2 * v] + bu)
        vm = cap_m * jnp.tanh(fm[2 * v + 1] + bv)
        ve = cap_e * jnp.tanh(fe[2 * v + 1] + bv)
        vel_ref[2 * v] = jnp.transpose(um[M:M + NX], (1, 0, 2))
        vel_ref[2 * v + 1] = jnp.transpose(vm[M:M + NX], (1, 0, 2))
        i = slice(1, EX - 1)
        fn_m, fn_e = shift(vm[i] * cos_m, ve[i] * cos_e, 1)
        fs_m, fs_e = shift(vm[i] * cos_m, ve[i] * cos_e, -1)

        def coef(u, vv, met, fn, fs):
            div = met * ((u[2:] - u[:-2]) * 0.5 + (fn - fs) * 0.5)
            up, un = met * jnp.maximum(u[i], 0.0), met * jnp.minimum(u[i], 0.0)
            vp, vn = jnp.maximum(vv[i], 0.0), jnp.minimum(vv[i], 0.0)
            return (un - up) + (vn - vp) - div, up, un, vp, vn

        cm = coef(um, vm, met_m, fn_m, fs_m)
        ce = coef(ue, ve, met_e, fn_e, fs_e)

        def rate(qm, qe, k):
            n = EX - 2 * k
            nm, ne = shift(qm[1:-1], qe[1:-1], 1)
            sm, se = shift(qm[1:-1], qe[1:-1], -1)

            def one(q, c, qn, qs):
                c0, up, un, vp, vn = (t[k - 1:k - 1 + n] for t in c)
                return c0 * q[1:-1] + up * q[:-2] - un * q[2:] + vp * qs - vn * qn
            return one(qm, cm, nm, sm), one(qe, ce, ne, se)

        qm = fm[NC + v]
        qe = fe[NC + v]
        r1m, r1e = rate(qm, qe, 1)
        tot = r1m[3:3 + NX]
        r2m, r2e = rate(qm[1:-1] + 0.25 * r1m, qe[1:-1] + 0.25 * r1e, 2)
        tot = tot + 2.0 * r2m[2:2 + NX]
        r3m, r3e = rate(qm[2:-2] + 0.25 * r2m, qe[2:-2] + 0.25 * r2e, 3)
        tot = tot + 2.0 * r3m[1:1 + NX]
        r4m, _ = rate(qm[3:-3] + 0.5 * r3m, qe[3:-3] + 0.5 * r3e, 4)
        tend_ref[v] = jnp.transpose((tot + r4m) * (1.0 / 6.0), (1, 0, 2))


def solution(mesh):
    n_lon, n_lat = mesh.shape["lon"], mesh.shape["lat"]
    tables = lat_tables(n_lat)

    def body(hidden_in, w1, b1, w2, b2, state):
        vmem = pl.BlockSpec(memory_space=pltpu.VMEM)
        dma = pltpu.SemaphoreType.DMA
        return pl.pallas_call(
            functools.partial(kernel, n_lon, n_lat),
            out_shape=(jax.ShapeDtypeStruct((NC, LV, NX, NY), F32),
                       jax.ShapeDtypeStruct((NV, LV, NX, NY), F32)),
            in_specs=[pl.BlockSpec(memory_space=pl.ANY), vmem, vmem, vmem,
                      pl.BlockSpec(memory_space=pltpu.SMEM), vmem, vmem],
            out_specs=(vmem, vmem),
            scratch_shapes=[
                pltpu.VMEM((LV, CH, NX, NY), BF16),
                pltpu.VMEM((LV, NX + 2, CH, NY), BF16),
                pltpu.VMEM((LV, NX, CH, NY), BF16),
                pltpu.VMEM((LV // 2, 3 * CH, 4 * CH), BF16),
                pltpu.VMEM((192, 2 * CH), BF16),
                pltpu.VMEM((NX, CH, 2 * NY), BF16),
                pltpu.VMEM((NX, CH, 2 * NY), BF16),
                pltpu.VMEM((CH, NY), F32),
                pltpu.VMEM((2, CH, NY), BF16),
                pltpu.VMEM((2, CH, NY), BF16),
                pltpu.VMEM((2, 2, CH, NY), BF16),
                pltpu.VMEM((NC * NR * LV, NY), F32),
                pltpu.VMEM((NC * NR * LV, NY), F32),
                pltpu.VMEM((NF, EX, LV, NY), F32),
                pltpu.VMEM((NF, EX, LV, NY), F32),
                pltpu.VMEM((2, NF, LV, NY), F32),
                pltpu.VMEM((2, NF, LV, NY), F32),
                pltpu.VMEM((2, NC, 5, LV, NY), F32),
                pltpu.VMEM((2, NF, LV, NY), F32),
                pltpu.VMEM((2, NF, LV, NY), F32),
                dma((LV,)), dma((2,)), dma((2,)), dma((4,)), dma((4,)),
                dma((2,)), dma((2,)), dma((4,)), dma((4,)),
                dma((2,)), dma((2,)), dma((4,)), dma((4,)),
            ],
            compiler_params=pltpu.CompilerParams(
                collective_id=0, has_side_effects=True, vmem_limit_bytes=60 * 1024 * 1024),
        )(hidden_in, w1, b1.reshape(1, CH), jnp.transpose(w2, (0, 1, 3, 2)), b2, state,
          jnp.asarray(tables))

    spread = P(None, None, "lon", "lat")
    return jax.shard_map(
        body, mesh=mesh, in_specs=(spread, P(), P(), P(), P(), spread),
        out_specs=(spread, spread), check_vma=False)
```

time: 191 us -> 79.4 us (0.42)
  Pallas kernels: 0 us -> 74.8 us
  local copies, waits for them, and re-layouts: 54.3 us -> 3.84 us
  waiting for transfers between devices: 43.8 us -> 0 us
  starting transfers between devices: 42.8 us -> 0 us
  matrix products: 31.1 us -> 0 us
  other arithmetic: 16.7 us -> 0 us
    pallas_call x0 -> x1, Pallas kernels: none -> 74.8 us  [body(): pl.pallas_call(functools.partial(kernel, n_lon, n_lat), out_shape=(jax.Sh...]
    ppermute x20 -> x0, waiting for transfers between devices: 43.8 us -> none  [the longest x2 14.5 us: padded_2(): lax.ppermute(lax.slice_in_dim(block, block.shape[dim] - width, None, axis...]
    ppermute x20 -> x0, starting transfers between devices: 42.8 us -> none  [the longest x8 16.3 us: with_halo(): lax.ppermute(leading, axis, [(b, a) for a, b in up])]
    dot_general x16 -> x0, matrix products: 31.1 us -> none  [conv_block(): jnp.einsum('tcxy,tco->oxy', taps, stacked, preferred_element_type=jnp.flo...]
    while x128 -> x0, local copies, waits for them, and re-layouts: 20.9 us -> none
    mul x14 -> x0, other arithmetic: 11.1 us -> none  [the longest x1 4.97 us: body(): padded = padded * lat_profile(in_width, lat_dev)[0].astype(jnp.bfloat16)]
    squeeze x8 -> x0, local copies, waits for them, and re-layouts: 9.44 us -> none  [body(): wide = jnp.transpose(lax.map(level, padded), (1, 0, 2, 3))]
    dynamic_update_slice x8 -> x0, local copies, waits for them, and re-layouts: 7.05 us -> none  [body(): wide = jnp.transpose(lax.map(level, padded), (1, 0, 2, 3))]
  transfers between devices with their start and end apart: 20 -> 0, of which waited for: 8 -> 0; matrix products, arithmetic and copies ran while one was open for 4% -> 0% of each run, Pallas kernels for 0% -> 0%
where the time goes in v1:
time: 79.4 us; the launch traced here: 79.2 us
  Pallas kernels  74.8 us (94%)
  local copies, waits for them, and re-layouts  3.84 us (5%)
    pallas_call x1, Pallas kernels, body(): pl.pallas_call(functools.partial(kernel, n_lon, n_lat), out_shape=(jax.Sh...  74.8 us
    unnamed x2, local copies, waits for them, and re-layouts  3.84 us

profile of v1, /device:TPU:1, one launch (start us, length us, event | category | flops | bytes accessed | tf_op | source)
XLA Modules:
  0.0 79.2 jit_solution(7083263925574820997)
XLA Ops:
  0.6 74.8 %shard_map.86 = (f32[12,8,16,128]{3,2,1,0:T(8,128)}, f32[6,8,16,128]{3,2,1,0:T(8,128)}) custom-call(bf16[8,128,16,128]{3,2,1,0:T(8,128)(2,1)} %x_hbm.1, bf16[3,3,128,128]{3,2,1,0:T(8,128)(2,1)} %w1_ref.1, f32[1,128]{1,0:T(1,128)} %bitcast.3, bf16[3,3,12,128]{3,2,1,0:T(8,128)(2,1)} %bitcast.2, f32[12]{0:T(128)} %b2_ref.1, f32[6,8,16,128]{3,2,1,0:T(8,128)} %st_ref.1, ...), custom_call_target="tpu_custom_call" | custom-call | tf_op jit(solution)/shard_map/pallas_call | solution.py:407
  75.4 2.1 %copy.11 = f32[12,8,16,128]{3,2,1,0:T(8,128)} copy(f32[12,8,16,128]{3,2,1,0:T(8,128)} %get-tuple-element.4) | data formatting | bytes 1572864
  77.5 1.8 %copy.12 = f32[6,8,16,128]{3,2,1,0:T(8,128)} copy(f32[6,8,16,128]{3,2,1,0:T(8,128)} %get-tuple-element.5) | data formatting | bytes 786432

commit v2 on v1

v2 whole, which is shorter than its diff:
```python
import functools
import math

import jax
import jax.numpy as jnp
import numpy as np
from jax import lax
from jax.experimental import pallas as pl
from jax.experimental.pallas import tpu as pltpu
from jax.sharding import PartitionSpec as P

MESH = pl.DeviceIdType.MESH
F32 = jnp.float32
BF16 = jnp.bfloat16
TIME_STEP = 0.5
SPEED_CAP = 0.6
COS_FLOOR = 0.5
NV = 6
NC = 12
NF = 18
LV = 8
NX = 16
NY = 128
CH = 128
M = 4
EX = NX + 2 * M
NR = NX + 2
NP = 2 * NC + NV
HALF = LV // 2


def lat_tables(n_lat_dev):
    n_lat = n_lat_dev * NY
    out = np.zeros((n_lat_dev, 2, LV, 2 * NY), np.float32)
    for d in range(n_lat_dev):
        lane = np.arange(2 * NY)
        y = np.where(lane < NY + NY // 2, lane, lane - 2 * NY) + d * NY
        phi = (y + 0.5) * (math.pi / n_lat) - 0.5 * math.pi
        inside = ((y >= 0) & (y < n_lat)).astype(np.float32)
        out[d, 0] = np.maximum(np.cos(phi), COS_FLOOR)[None]
        out[d, 1] = (SPEED_CAP * inside)[None]
    return out


def lanes(shape):
    return lax.broadcasted_iota(jnp.int32, shape, len(shape) - 1)


def roll(v, s):
    s = s % NY
    return v if s == 0 else pltpu.roll(v, s, v.ndim - 1)


def kernel(n_lon, n_lat, x_hbm, w1_ref, b1_ref, w2_ref, b2_ref, st_ref, tab_ref,
           vel_ref, tend_ref,
           xin, xt, ht, lhs1, lhs2, oh, ohe, bias, xe, xh, xc, pm, pe, fm, fe, pk, pr, rowr, epk, epr,
           in_sem, x_s, x_r, row_s, row_r, cor_s, cor_r, lat_s, lat_r, lon_s, lon_r, q_s, q_r):
    lon = lax.axis_index("lon")
    lat = lax.axis_index("lat")
    left = (lax.rem(lon + n_lon - 1, n_lon), lat)
    right = (lax.rem(lon + 1, n_lon), lat)
    south = (lon, lat - 1)
    north = (lon, lat + 1)
    has_s = lat > 0
    has_n = lat < n_lat - 1

    for side, has in ((0, has_s), (1, has_n)):
        @pl.when(jnp.logical_not(has))
        def _():
            xh[side] = jnp.zeros((CH, NY), BF16)
            pr[side] = jnp.zeros((NP, LV, NY), F32)

    barrier = pltpu.get_barrier_semaphore()
    for dev in (left, right):
        pl.semaphore_signal(barrier, inc=1, device_id=dev, device_id_type=MESH)

    @pl.when(has_s)
    def _():
        pl.semaphore_signal(barrier, inc=1, device_id=south, device_id_type=MESH)

    @pl.when(has_n)
    def _():
        pl.semaphore_signal(barrier, inc=1, device_id=north, device_id_type=MESH)

    loads = [pltpu.make_async_copy(x_hbm.at[l], xin.at[l], in_sem.at[l]) for l in range(LV)]
    for c in loads:
        c.start()

    for b in range(3):
        for a in range(3):
            lhs1[0, b * CH:(b + 1) * CH, a * CH:(a + 1) * CH] = jnp.transpose(w1_ref[a, b], (1, 0))
    for lp in range(1, LV // 2):
        lhs1[lp, :, 0:3 * CH] = lhs1[0, :, 0:3 * CH]
    lhs2[...] = jnp.zeros_like(lhs2)
    for b in range(3):
        for off in range(4):
            for r in range(2):
                a = r - off + 2
                if 0 <= a <= 2:
                    base = b * 64 + off * 16
                    lhs2[base:base + NC, r * CH:(r + 1) * CH] = w2_ref[a, b]
    bias[...] = jnp.transpose(jnp.broadcast_to(b1_ref[...], (CH, CH)), (1, 0))
    k_id = lax.broadcasted_iota(jnp.int32, (CH, 2 * NY), 0)
    lane2 = lanes((CH, 2 * NY))
    half = (k_id // 16) % 2
    target = half * NY + jnp.where(k_id < 64, 0, NY - 1)
    hit = lane2 == target

    @pl.loop(0, NX)
    def _(x):
        oh[x] = jnp.where(hit & (k_id % 16 == x), 1.0, 0.0).astype(BF16)
        want_hi = (k_id == NY - 1) & (lane2 == x)
        want_lo = (k_id == 0) & (lane2 == NY + x)
        ohe[x] = jnp.where(want_hi | want_lo, 1.0, 0.0).astype(BF16)

    ht[:, 0] = jnp.zeros((LV, CH, NY), BF16)
    ht[:, NX + 1] = jnp.zeros((LV, CH, NY), BF16)

    def rcopy(src, dst, ss, rs_, dev):
        return pltpu.make_async_remote_copy(src_ref=src, dst_ref=dst, send_sem=ss, recv_sem=rs_,
                                            device_id=dev, device_id_type=MESH)

    hi = jnp.zeros((CH, NY), F32)
    lo = jnp.zeros((CH, NY), F32)
    rows_left, rows_right = [], []
    for l in range(LV):
        loads[l].wait()
        xt[l, 1:NX + 1] = jnp.transpose(xin[l], (1, 0, 2))
        row = jnp.concatenate([xt[l, 1 + x] for x in range(NX)], axis=1)
        res = jnp.dot(row, ohe[...].reshape(NX * NY, 2 * NY), preferred_element_type=F32)
        hi = hi + roll(res[:, :NY], 16 * l)
        lo = lo + roll(res[:, NY:], 16 * l)
        if l == HALF - 1:
            pl.semaphore_wait(barrier, 2 + has_s.astype(jnp.int32) + has_n.astype(jnp.int32))
        if (l + 1) % HALF == 0:
            g = l // HALF
            part = slice(g * HALF, (g + 1) * HALF)
            rows_left.append(rcopy(xt.at[part, 1], xt.at[part, NX + 1], row_s.at[g], row_r.at[g], left))
            rows_right.append(rcopy(xt.at[part, NX], xt.at[part, 0], row_s.at[2 + g], row_r.at[2 + g], right))
            rows_left[-1].start()
            rows_right[-1].start()
    xe[0] = hi.astype(BF16)
    xe[1] = lo.astype(BF16)

    def lat_exchange(src_n, src_s, dst_from_s, dst_from_n, sems, semr, at):
        to_n = rcopy(src_n, dst_from_s, sems.at[at], semr.at[at], north)
        to_s = rcopy(src_s, dst_from_n, sems.at[at + 1], semr.at[at + 1], south)

        @pl.when(has_n)
        def _():
            to_n.start()

        @pl.when(has_s)
        def _():
            to_s.start()

        def finish():
            @pl.when(has_s)
            def _():
                to_n.wait_recv()
                to_s.wait_send()

            @pl.when(has_n)
            def _():
                to_s.wait_recv()
                to_n.wait_send()
        return finish

    lane8 = lanes((LV, NY))

    def pack_lat(slot, cells):
        to_n = jnp.zeros((LV, NY), F32)
        to_s = jnp.zeros((LV, NY), F32)
        for i, (m, e) in enumerate(cells):
            mine = (lane8 >= 5 * i) & (lane8 < 5 * i + 5)
            to_n = jnp.where(mine, roll(jnp.where(lane8 == 0, e, m), 5 * i + 4), to_n)
            to_s = jnp.where(mine, roll(jnp.where(lane8 == NY - 1, e, m), 5 * i + 1), to_s)
        pk[0, slot] = to_n
        pk[1, slot] = to_s

    def send_lat(lo_, hi_, at):
        return lat_exchange(pk.at[0, lo_:hi_], pk.at[1, lo_:hi_], pr.at[0, lo_:hi_], pr.at[1, lo_:hi_],
                            lat_s, lat_r, at)

    def from_lat(slot, i):
        a = roll(pr[0, slot], -(5 * i + 4))
        b = roll(pr[1, slot], -(5 * i + 1))
        fix = jnp.where(lane8 == 0, a, jnp.where(lane8 == NY - 1, b, 0.0))
        ext = jnp.where(lane8 >= NY - 4, a, jnp.where(lane8 < 4, b, 0.0))
        return fix, ext

    def pack_rows(exts, fixes):
        acc = jnp.zeros((LV, NY), F32)
        for r in range(len(exts)):
            acc = jnp.where((lane8 >= 8 * r) & (lane8 < 8 * r + 8), roll(exts[r], 8 * r + 4), acc)
        for r in range(len(fixes)):
            acc = jnp.where((lane8 >= 40 + 2 * r) & (lane8 < 42 + 2 * r), roll(fixes[r], 41 + 2 * r), acc)
        return acc

    x_lat = lat_exchange(xe.at[0], xe.at[1], xh.at[0], xh.at[1], x_s, x_r, 0)

    zero8 = jnp.zeros((LV, NY), F32)
    for v in range(NV):
        fm[NC + v, M:M + NX] = jnp.transpose(st_ref[v], (1, 0, 2))

    @pl.loop(0, NV)
    def _(v):
        pack_lat(2 * NC + v, [(fm[NC + v, M + x], zero8) for x in range(NX)])

    q_lat = send_lat(2 * NC, NP, 4)

    x_lat()
    c_left = rcopy(xh, xc.at[1], cor_s.at[0], cor_r.at[0], left)
    c_right = rcopy(xh, xc.at[0], cor_s.at[1], cor_r.at[1], right)
    c_left.start()
    c_right.start()

    def inject(corners):
        xpos = lanes((CH, NY)) % NX
        kinds = []
        for side in range(2):
            b = 2 * side
            own = xh[side].astype(F32)
            t0, t2 = roll(own, 1), roll(own, -1)
            if corners:
                t0 = jnp.where(xpos == 0, roll(xc[0, side].astype(F32), -(NX - 1)), t0)
                t2 = jnp.where(xpos == NX - 1, roll(xc[1, side].astype(F32), NX - 1), t2)
            taps = jnp.concatenate([t0.astype(BF16), xh[side], t2.astype(BF16)], axis=0)
            e = jnp.dot(lhs1[0, b * CH:(b + 1) * CH, 0:3 * CH], taps, preferred_element_type=F32)
            e_hi = e.astype(BF16).astype(F32)
            kinds += [e_hi, e - e_hi]
        group = lanes((CH, NY)) // 32
        for lp in range(LV // 2):
            inj = jnp.zeros((CH, NY), F32)
            for kind in range(4):
                inj = jnp.where(group == kind, roll(kinds[kind], 32 * kind - 32 * lp), inj)
            lhs1[lp, CH:2 * CH, 3 * CH:] = inj.astype(BF16)
            if not corners:
                lhs1[lp, 0:CH, 3 * CH:] = jnp.zeros((CH, NY), BF16)
                lhs1[lp, 2 * CH:, 3 * CH:] = jnp.zeros((CH, NY), BF16)

    inject(False)

    q_lat()

    @pl.loop(0, NV)
    def _(v):
        exts = []
        for x in range(NX):
            _, ext = from_lat(2 * NC + v, x)
            fe[NC + v, M + x] = ext
            exts.append(ext)
        epk[0, NC + v] = pack_rows(exts[:4], [])
        epk[1, NC + v] = pack_rows(exts[-4:], [])

    q_copies = [
        rcopy(fm.at[NC:NF, M:M + 4], fm.at[NC:NF, M + NX:M + NX + 4], q_s.at[0], q_r.at[0], left),
        rcopy(fm.at[NC:NF, M + NX - 4:M + NX], fm.at[NC:NF, 0:4], q_s.at[1], q_r.at[1], right),
        rcopy(epk.at[0, NC:NF], epr.at[1, NC:NF], q_s.at[2], q_r.at[2], left),
        rcopy(epk.at[1, NC:NF], epr.at[0, NC:NF], q_s.at[3], q_r.at[3], right)]
    for c in q_copies:
        c.start()

    lane1 = lanes((CH, NY))

    def conv1(lp, x):
        rhs = jnp.concatenate(
            [xt[2 * lp + h, pl.ds(x, 3)].reshape(3 * CH, NY) for h in range(2)], axis=1)
        rhs = jnp.concatenate([rhs, oh[x]], axis=0)
        s = jnp.dot(lhs1[lp], rhs, preferred_element_type=F32)
        for h in range(2):
            c = slice(h * NY, (h + 1) * NY)
            pre = s[CH:2 * CH, c] + bias[...]
            pre = pre + jnp.where(lane1 == 0, 0.0, roll(s[0:CH, c], 1))
            pre = pre + jnp.where(lane1 == NY - 1, 0.0, roll(s[2 * CH:, c], -1))
            half_pre = 0.5 * pre
            ht[2 * lp + h, x + 1] = (half_pre + half_pre * jnp.tanh(half_pre)).astype(BF16)

    lane64 = lanes((64, NY))

    def conv2(lp, j):
        rhs = jnp.concatenate(
            [ht[2 * lp + h, 2 * j:2 * j + 2].reshape(2 * CH, NY) for h in range(2)], axis=1)
        s = jnp.dot(lhs2[...], rhs, preferred_element_type=F32)
        out = []
        for h in range(2):
            c = slice(h * NY, (h + 1) * NY)
            up = roll(s[0:64, c], 1)
            dn = roll(s[128:192, c], -1)
            main = s[64:128, c] + jnp.where(lane64 == 0, 0.0, up) + jnp.where(lane64 == NY - 1, 0.0, dn)
            edge = jnp.where(lane64 == 0, up, 0.0) + jnp.where(lane64 == NY - 1, dn, 0.0)
            out.append((main, edge))
        return out

    def put(lp, row, parts, more=False):
        for h in range(2):
            at = pl.ds(row * (NC * LV) + 2 * lp + h, NC, stride=LV)
            for k, ref in enumerate((pm, pe)):
                t = None
                for pair, off in parts:
                    piece = pair[h][k][off * 16:off * 16 + NC]
                    t = piece if t is None else t + piece
                ref[at, :] = ref[at, :] + t if more else t

    def cell(row, f):
        at = pl.ds(pl.multiple_of((row * NC + f) * LV, LV), LV)
        return pm[at, :], pe[at, :]

    @pl.loop(0, LV)
    def _(i):
        lp, g = i // 2, i % 2
        for u in range(4):
            conv1(lp, 1 + 10 * g + u)

    for c in (c_left, c_right, *rows_left, *rows_right):
        c.wait()
    inject(True)

    @pl.loop(0, LV // 4)
    def _(i):
        for u in range(2):
            conv1(2 * i + u, 0)
            conv1(2 * i + u, NX - 1)

    @pl.loop(0, LV // 2)
    def _(lp):
        p = [conv2(lp, j) for j in range(3)]
        put(lp, 0, [(p[0], 1)])
        for i in range(2):
            put(lp, 1 + i, [(p[0], 2 + i), (p[1], i)])
            put(lp, 3 + i, [(p[1], 2 + i), (p[2], i)])
            put(lp, 5 + i, [(p[2], 2 + i)])
        p = [conv2(lp, j) for j in range(6, 9)]
        for i in range(2):
            put(lp, 11 + i, [(p[0], i)])
            put(lp, 13 + i, [(p[0], 2 + i), (p[1], i)])
            put(lp, 15 + i, [(p[1], 2 + i), (p[2], i)])
        put(lp, 17, [(p[2], 2)])

    span = 5 * NC * LV
    r_left = rcopy(pm.at[0:span], rowr.at[1], lon_s.at[0], lon_r.at[0], left)
    r_right = rcopy(pm.at[(NR - 5) * NC * LV:NR * NC * LV], rowr.at[0], lon_s.at[1], lon_r.at[1], right)
    r_left.start()
    r_right.start()

    outer = [0, 1, 2, 3, 4, NR - 5, NR - 4, NR - 3, NR - 2, NR - 1]
    inner = list(range(5, NR - 5))

    @pl.loop(0, NC)
    def _(f):
        pack_lat(f, [cell(r, f) for r in outer])

    outer_lat = send_lat(0, NC, 0)

    @pl.loop(0, LV // 2)
    def _(lp):
        for x in range(5, NX - 5):
            conv1(lp, x)

    outer_lat()

    def take(slot, i, row, f):
        m, e = cell(row, f)
        fix, ext = from_lat(slot, i)
        fm[f, M - 1 + row] = m + fix
        fe[f, M - 1 + row] = e + ext
        return fix, e + ext

    @pl.loop(0, NC)
    def _(f):
        got = [take(f, i, r, f) for i, r in enumerate(outer)]
        epk[0, f] = pack_rows([g[1] for g in got[:5]], [g[0] for g in got[:5]])
        epk[1, f] = pack_rows([g[1] for g in got[5:]], [g[0] for g in got[5:]])

    e_left = rcopy(epk.at[0, 0:NC], epr.at[1, 0:NC], lon_s.at[2], lon_r.at[2], left)
    e_right = rcopy(epk.at[1, 0:NC], epr.at[0, 0:NC], lon_s.at[3], lon_r.at[3], right)
    e_left.start()
    e_right.start()

    @pl.loop(0, LV // 2)
    def _(lp):
        p = [conv2(lp, j) for j in range(3, 6)]
        for i in range(2):
            put(lp, 5 + i, [(p[0], i)], True)
            put(lp, 7 + i, [(p[0], 2 + i), (p[1], i)])
            put(lp, 9 + i, [(p[1], 2 + i), (p[2], i)])
            put(lp, 11 + i, [(p[2], 2 + i)], True)

    @pl.loop(0, NC)
    def _(f):
        pack_lat(NC + f, [cell(r, f) for r in inner])

    inner_lat = send_lat(NC, 2 * NC, 2)

    for c in q_copies:
        c.wait()

    def ext_lanes(t):
        return jnp.where((lane8 < 4) | (lane8 >= NY - 4), t, 0.0)

    @pl.loop(NC, NF)
    def _(f):
        for side in range(2):
            t = epr[side, f]
            for r in range(4):
                fe[f, (0 if side == 0 else M + NX) + r] = ext_lanes(roll(t, -(8 * r + 4)))

    inner_lat()

    @pl.loop(0, NC)
    def _(f):
        for i, r in enumerate(inner):
            take(NC + f, i, r, f)

    for c in (r_left, r_right, e_left, e_right):
        c.wait()

    @pl.loop(0, NC)
    def _(f):
        for side in range(2):
            t = epr[side, f]
            for r in range(5):
                x = (r if side == 0 else M + NX - 1 + r)
                fix = jnp.where((lane8 == 0) | (lane8 == NY - 1), roll(t, -(41 + 2 * r)), 0.0)
                got = rowr[side, pl.ds(pl.multiple_of((r * NC + f) * LV, LV), LV), :] + fix
                ext = ext_lanes(roll(t, -(8 * r + 4)))
                if x < M - 1 or x > M + NX:
                    fm[f, x] = got
                    fe[f, x] = ext
                else:
                    fm[f, x] = fm[f, x] + got
                    fe[f, x] = fe[f, x] + ext

    cos_m = tab_ref[lat, 0, :, 0:NY]
    cos_e = tab_ref[lat, 0, :, NY:]
    cap_m = tab_ref[lat, 1, :, 0:NY]
    cap_e = tab_ref[lat, 1, :, NY:]
    met_m = 1.0 / cos_m
    met_e = 1.0 / cos_e

    def shift(m, e, step):
        sh = 1 if step < 0 else -1
        edge = 0 if step < 0 else NY - 1
        rm, re = roll(m, sh), roll(e, sh)
        at = lanes(m.shape) == edge
        return jnp.where(at, re, rm), jnp.where(at, rm, re)

    @pl.loop(0, NV)
    def _(v):
        bu = b2_ref[2 * v]
        bv = b2_ref[2 * v + 1]
        um = cap_m * jnp.tanh(fm[2 * v] + bu)
        ue = cap_e * jnp.tanh(fe[2 * v] + bu)
        vm = cap_m * jnp.tanh(fm[2 * v + 1] + bv)
        ve = cap_e * jnp.tanh(fe[2 * v + 1] + bv)
        vel_ref[2 * v] = um[M:M + NX]
        vel_ref[2 * v + 1] = vm[M:M + NX]
        i = slice(1, EX - 1)
        fn_m, fn_e = shift(vm[i] * cos_m, ve[i] * cos_e, 1)
        fs_m, fs_e = shift(vm[i] * cos_m, ve[i] * cos_e, -1)

        def coef(u, vv, met, fn, fs):
            div = met * ((u[2:] - u[:-2]) * 0.5 + (fn - fs) * 0.5)
            up, un = met * jnp.maximum(u[i], 0.0), met * jnp.minimum(u[i], 0.0)
            vp, vn = jnp.maximum(vv[i], 0.0), jnp.minimum(vv[i], 0.0)
            return (un - up) + (vn - vp) - div, up, un, vp, vn

        cm = coef(um, vm, met_m, fn_m, fs_m)
        ce = coef(ue, ve, met_e, fn_e, fs_e)

        def rate(qm, qe, k):
            n = EX - 2 * k
            nm, ne = shift(qm[1:-1], qe[1:-1], 1)
            sm, se = shift(qm[1:-1], qe[1:-1], -1)

            def one(q, c, qn, qs):
                c0, up, un, vp, vn = (t[k - 1:k - 1 + n] for t in c)
                return c0 * q[1:-1] + up * q[:-2] - un * q[2:] + vp * qs - vn * qn
            return one(qm, cm, nm, sm), one(qe, ce, ne, se)

        qm = fm[NC + v]
        qe = fe[NC + v]
        r1m, r1e = rate(qm, qe, 1)
        tot = r1m[3:3 + NX]
        r2m, r2e = rate(qm[1:-1] + 0.25 * r1m, qe[1:-1] + 0.25 * r1e, 2)
        tot = tot + 2.0 * r2m[2:2 + NX]
        r3m, r3e = rate(qm[2:-2] + 0.25 * r2m, qe[2:-2] + 0.25 * r2e, 3)
        tot = tot + 2.0 * r3m[1:1 + NX]
        r4m, _ = rate(qm[3:-3] + 0.5 * r3m, qe[3:-3] + 0.5 * r3e, 4)
        tend_ref[v] = (tot + r4m) * (1.0 / 6.0)


def solution(mesh):
    n_lon, n_lat = mesh.shape["lon"], mesh.shape["lat"]
    tables = lat_tables(n_lat)

    def body(hidden_in, w1, b1, w2, b2, state):
        vmem = pl.BlockSpec(memory_space=pltpu.VMEM)
        dma = pltpu.SemaphoreType.DMA
        vel, tend = pl.pallas_call(
            functools.partial(kernel, n_lon, n_lat),
            out_shape=(jax.ShapeDtypeStruct((NC, NX, LV, NY), F32),
                       jax.ShapeDtypeStruct((NV, NX, LV, NY), F32)),
            in_specs=[pl.BlockSpec(memory_space=pl.ANY), vmem, vmem, vmem,
                      pl.BlockSpec(memory_space=pltpu.SMEM), vmem, vmem],
            out_specs=(vmem, vmem),
            scratch_shapes=[
                pltpu.VMEM((LV, CH, NX, NY), BF16),
                pltpu.VMEM((LV, NX + 2, CH, NY), BF16),
                pltpu.VMEM((LV, NX + 2, CH, NY), BF16),
                pltpu.VMEM((LV // 2, 3 * CH, 4 * CH), BF16),
                pltpu.VMEM((192, 2 * CH), BF16),
                pltpu.VMEM((NX, CH, 2 * NY), BF16),
                pltpu.VMEM((NX, CH, 2 * NY), BF16),
                pltpu.VMEM((CH, NY), F32),
                pltpu.VMEM((2, CH, NY), BF16),
                pltpu.VMEM((2, CH, NY), BF16),
                pltpu.VMEM((2, 2, CH, NY), BF16),
                pltpu.VMEM((NR * NC * LV, NY), F32),
                pltpu.VMEM((NR * NC * LV, NY), F32),
                pltpu.VMEM((NF, EX, LV, NY), F32),
                pltpu.VMEM((NF, EX, LV, NY), F32),
                pltpu.VMEM((2, NP, LV, NY), F32),
                pltpu.VMEM((2, NP, LV, NY), F32),
                pltpu.VMEM((2, 5 * NC * LV, NY), F32),
                pltpu.VMEM((2, NF, LV, NY), F32),
                pltpu.VMEM((2, NF, LV, NY), F32),
                dma((LV,)), dma((2,)), dma((2,)), dma((4,)), dma((4,)), dma((2,)), dma((2,)),
                dma((6,)), dma((6,)), dma((4,)), dma((4,)), dma((4,)), dma((4,)),
            ],
            compiler_params=pltpu.CompilerParams(
                collective_id=0, has_side_effects=True, vmem_limit_bytes=55 * 1024 * 1024),
        )(hidden_in, w1, b1.reshape(1, CH), jnp.transpose(w2, (0, 1, 3, 2)), b2, state,
          jnp.asarray(tables))
        return jnp.transpose(vel, (0, 2, 1, 3)), jnp.transpose(tend, (0, 2, 1, 3))

    spread = P(None, None, "lon", "lat")
    return jax.shard_map(
        body, mesh=mesh, in_specs=(spread, P(), P(), P(), P(), spread),
        out_specs=(spread, spread), check_vma=False)
```

time: 79.4 us -> 59.2 us (0.75)
  the two profiles are of different devices: /device:TPU:1 before, /device:TPU:25 now
where the time goes in v2:
time: 59.2 us; the launch traced here: 59 us
  Pallas kernels  54.4 us (92%)
  local copies, waits for them, and re-layouts  3.96 us (7%)
  between operations  0.64 us (1%)
    pallas_call x1, Pallas kernels, body(): pl.pallas_call(functools.partial(kernel, n_lon, n_lat), out_shape=(jax.Sh...  54.4 us
    unnamed x2, local copies, waits for them, and re-layouts  3.96 us

profile of v2, /device:TPU:25, one launch (start us, length us, event | category | flops | bytes accessed | tf_op | source)
XLA Modules:
  0.0 59.0 jit_solution(10833436700142617683)
XLA Ops:
  0.6 54.4 %shard_map.86 = (f32[12,16,8,128]{3,2,1,0:T(8,128)}, f32[6,16,8,128]{3,2,1,0:T(8,128)}) custom-call(bf16[8,128,16,128]{3,2,1,0:T(8,128)(2,1)} %x_hbm.1, bf16[3,3,128,128]{3,2,1,0:T(8,128)(2,1)} %w1_ref.1, f32[1,128]{1,0:T(1,128)} %bitcast.7, bf16[3,3,12,128]{3,2,1,0:T(8,128)(2,1)} %bitcast.6, f32[12]{0:T(128)} %b2_ref.1, f32[6,8,16,128]{3,2,1,0:T(8,128)} %st_ref.1, ...), custom_call_target="tpu_custom_call" | custom-call | tf_op jit(solution)/shard_map/pallas_call | solution.py:500
  55.0 2.2 %copy.9 = f32[12,8,16,128]{3,2,1,0:T(8,128)} copy(f32[12,8,16,128]{3,1,2,0:T(8,128)} %bitcast.4) | data formatting | bytes 1572864
  57.2 1.8 %copy.10 = f32[6,8,16,128]{3,2,1,0:T(8,128)} copy(f32[6,8,16,128]{3,1,2,0:T(8,128)} %bitcast.5) | data formatting | bytes 786432

commit v3 on v2

--- a/solution.py
+++ b/solution.py
@@ -126,10 +126,13 @@
     for l in range(LV):
         loads[l].wait()
         xt[l, 1:NX + 1] = jnp.transpose(xin[l], (1, 0, 2))
-        row = jnp.concatenate([xt[l, 1 + x] for x in range(NX)], axis=1)
-        res = jnp.dot(row, ohe[...].reshape(NX * NY, 2 * NY), preferred_element_type=F32)
-        hi = hi + roll(res[:, :NY], 16 * l)
-        lo = lo + roll(res[:, NY:], 16 * l)
+        if l % 2 == 1:
+            row = jnp.concatenate(
+                [jnp.concatenate([xt[l - 1 + h, 1 + x] for x in range(NX)], axis=1) for h in range(2)], axis=0)
+            res = jnp.dot(row, ohe[...].reshape(NX * NY, 2 * NY), preferred_element_type=F32)
+            for h in range(2):
+                hi = hi + roll(res[h * CH:(h + 1) * CH, :NY], 16 * (l - 1 + h))
+                lo = lo + roll(res[h * CH:(h + 1) * CH, NY:], 16 * (l - 1 + h))
         if l == HALF - 1:
             pl.semaphore_wait(barrier, 2 + has_s.astype(jnp.int32) + has_n.astype(jnp.int32))
         if (l + 1) % HALF == 0:
@@ -137,8 +140,9 @@
             part = slice(g * HALF, (g + 1) * HALF)
             rows_left.append(rcopy(xt.at[part, 1], xt.at[part, NX + 1], row_s.at[g], row_r.at[g], left))
             rows_right.append(rcopy(xt.at[part, NX], xt.at[part, 0], row_s.at[2 + g], row_r.at[2 + g], right))
-            rows_left[-1].start()
-            rows_right[-1].start()
+            if g == 0:
+                rows_left[0].start()
+                rows_right[0].start()
     xe[0] = hi.astype(BF16)
     xe[1] = lo.astype(BF16)
 
@@ -203,17 +207,22 @@
     for v in range(NV):
         fm[NC + v, M:M + NX] = jnp.transpose(st_ref[v], (1, 0, 2))
 
-    @pl.loop(0, NV)
+    @pl.loop(0, NV, unroll=2)
     def _(v):
         pack_lat(2 * NC + v, [(fm[NC + v, M + x], zero8) for x in range(NX)])
-
-    q_lat = send_lat(2 * NC, NP, 4)
 
     x_lat()
     c_left = rcopy(xh, xc.at[1], cor_s.at[0], cor_r.at[0], left)
     c_right = rcopy(xh, xc.at[0], cor_s.at[1], cor_r.at[1], right)
     c_left.start()
     c_right.start()
+    rows_left[1].start()
+    rows_right[1].start()
+    q_copies = [
+        rcopy(fm.at[NC:NF, M:M + 4], fm.at[NC:NF, M + NX:M + NX + 4], q_s.at[0], q_r.at[0], left),
+        rcopy(fm.at[NC:NF, M + NX - 4:M + NX], fm.at[NC:NF, 0:4], q_s.at[1], q_r.at[1], right)]
+    for c in q_copies:
+        c.start()
 
     def inject(corners):
         xpos = lanes((CH, NY)) % NX
@@ -241,25 +250,7 @@
 
     inject(False)
 
-    q_lat()
-
-    @pl.loop(0, NV)
-    def _(v):
-        exts = []
-        for x in range(NX):
-            _, ext = from_lat(2 * NC + v, x)
-            fe[NC + v, M + x] = ext
-            exts.append(ext)
-        epk[0, NC + v] = pack_rows(exts[:4], [])
-        epk[1, NC + v] = pack_rows(exts[-4:], [])
-
-    q_copies = [
-        rcopy(fm.at[NC:NF, M:M + 4], fm.at[NC:NF, M + NX:M + NX + 4], q_s.at[0], q_r.at[0], left),
-        rcopy(fm.at[NC:NF, M + NX - 4:M + NX], fm.at[NC:NF, 0:4], q_s.at[1], q_r.at[1], right),
-        rcopy(epk.at[0, NC:NF], epr.at[1, NC:NF], q_s.at[2], q_r.at[2], left),
-        rcopy(epk.at[1, NC:NF], epr.at[0, NC:NF], q_s.at[3], q_r.at[3], right)]
-    for c in q_copies:
-        c.start()
+    q_lat = send_lat(2 * NC, NP, 4)
 
     lane1 = lanes((CH, NY))
 
@@ -321,6 +312,24 @@
         for u in range(2):
             conv1(2 * i + u, 0)
             conv1(2 * i + u, NX - 1)
+
+    q_lat()
+
+    @pl.loop(0, NV, unroll=2)
+    def _(v):
+        exts = []
+        for x in range(NX):
+            _, ext = from_lat(2 * NC + v, x)
+            fe[NC + v, M + x] = ext
+            exts.append(ext)
+        epk[0, NC + v] = pack_rows(exts[:4], [])
+        epk[1, NC + v] = pack_rows(exts[-4:], [])
+
+    q_edges = [
+        rcopy(epk.at[0, NC:NF], epr.at[1, NC:NF], q_s.at[2], q_r.at[2], left),
+        rcopy(epk.at[1, NC:NF], epr.at[0, NC:NF], q_s.at[3], q_r.at[3], right)]
+    for c in q_edges:
+        c.start()
 
     @pl.loop(0, LV // 2)
     def _(lp):
@@ -337,16 +346,21 @@
             put(lp, 15 + i, [(p[1], 2 + i), (p[2], i)])
         put(lp, 17, [(p[2], 2)])
 
-    span = 5 * NC * LV
-    r_left = rcopy(pm.at[0:span], rowr.at[1], lon_s.at[0], lon_r.at[0], left)
-    r_right = rcopy(pm.at[(NR - 5) * NC * LV:NR * NC * LV], rowr.at[0], lon_s.at[1], lon_r.at[1], right)
-    r_left.start()
-    r_right.start()
+    def rows_part(k, lo_, hi_):
+        at, to = pl.ds(lo_ * NC * LV, (hi_ - lo_) * NC * LV), NR - 5
+        far = pl.ds((to + lo_) * NC * LV, (hi_ - lo_) * NC * LV)
+        return [rcopy(pm.at[at], rowr.at[1, at], lon_s.at[k], lon_r.at[k], left),
+                rcopy(pm.at[far], rowr.at[0, at], lon_s.at[k + 1], lon_r.at[k + 1], right)]
+
+    first_rows = rows_part(0, 0, 2)
+    last_rows = rows_part(4, 2, 5)
+    for c in first_rows:
+        c.start()
 
     outer = [0, 1, 2, 3, 4, NR - 5, NR - 4, NR - 3, NR - 2, NR - 1]
     inner = list(range(5, NR - 5))
 
-    @pl.loop(0, NC)
+    @pl.loop(0, NC, unroll=2)
     def _(f):
         pack_lat(f, [cell(r, f) for r in outer])
 
@@ -354,10 +368,18 @@
 
     @pl.loop(0, LV // 2)
     def _(lp):
-        for x in range(5, NX - 5):
+        for x in range(5, NX - 7):
             conv1(lp, x)
 
     outer_lat()
+    for c in last_rows:
+        c.start()
+
+    @pl.loop(0, LV // 4)
+    def _(i):
+        for u in range(2):
+            for x in range(NX - 7, NX - 5):
+                conv1(2 * i + u, x)
 
     def take(slot, i, row, f):
         m, e = cell(row, f)
@@ -366,7 +388,7 @@
         fe[f, M - 1 + row] = e + ext
         return fix, e + ext
 
-    @pl.loop(0, NC)
+    @pl.loop(0, NC, unroll=2)
     def _(f):
         got = [take(f, i, r, f) for i, r in enumerate(outer)]
         epk[0, f] = pack_rows([g[1] for g in got[:5]], [g[0] for g in got[:5]])
@@ -386,13 +408,13 @@
             put(lp, 9 + i, [(p[1], 2 + i), (p[2], i)])
             put(lp, 11 + i, [(p[2], 2 + i)], True)
 
-    @pl.loop(0, NC)
+    @pl.loop(0, NC, unroll=2)
     def _(f):
         pack_lat(NC + f, [cell(r, f) for r in inner])
 
     inner_lat = send_lat(NC, 2 * NC, 2)
 
-    for c in q_copies:
+    for c in (*q_copies, *q_edges):
         c.wait()
 
     def ext_lanes(t):
@@ -407,15 +429,15 @@
 
     inner_lat()
 
-    @pl.loop(0, NC)
+    @pl.loop(0, NC, unroll=2)
     def _(f):
         for i, r in enumerate(inner):
             take(NC + f, i, r, f)
 
-    for c in (r_left, r_right, e_left, e_right):
+    for c in (*first_rows, *last_rows, e_left, e_right):
         c.wait()
 
-    @pl.loop(0, NC)
+    @pl.loop(0, NC, unroll=2)
     def _(f):
         for side in range(2):
             t = epr[side, f]
@@ -526,7 +548,7 @@
                 pltpu.VMEM((2, NF, LV, NY), F32),
                 pltpu.VMEM((2, NF, LV, NY), F32),
                 dma((LV,)), dma((2,)), dma((2,)), dma((4,)), dma((4,)), dma((2,)), dma((2,)),
-                dma((6,)), dma((6,)), dma((4,)), dma((4,)), dma((4,)), dma((4,)),
+                dma((6,)), dma((6,)), dma((6,)), dma((6,)), dma((4,)), dma((4,)),
             ],
             compiler_params=pltpu.CompilerParams(
                 collective_id=0, has_side_effects=True, vmem_limit_bytes=55 * 1024 * 1024),

time: 59.2 us -> 52.8 us (0.89)
  the two profiles are of different devices: /device:TPU:25 before, /device:TPU:1 now
where the time goes in v3:
time: 52.8 us; the launch traced here: 52.6 us
  Pallas kernels  48 us (91%)
  local copies, waits for them, and re-layouts  3.96 us (8%)
  between operations  0.64 us (1%)
    pallas_call x1, Pallas kernels, body(): pl.pallas_call(functools.partial(kernel, n_lon, n_lat), out_shape=(jax.Sh...  48 us
    unnamed x2, local copies, waits for them, and re-layouts  3.96 us

profile of v3, /device:TPU:1, one launch (start us, length us, event | category | flops | bytes accessed | tf_op | source)
XLA Modules:
  0.0 52.6 jit_solution(4965368596998171169)
XLA Ops:
  0.6 48.0 %shard_map.86 = (f32[12,16,8,128]{3,2,1,0:T(8,128)}, f32[6,16,8,128]{3,2,1,0:T(8,128)}) custom-call(bf16[8,128,16,128]{3,2,1,0:T(8,128)(2,1)} %x_hbm.1, bf16[3,3,128,128]{3,2,1,0:T(8,128)(2,1)} %w1_ref.1, f32[1,128]{1,0:T(1,128)} %bitcast.7, bf16[3,3,12,128]{3,2,1,0:T(8,128)(2,1)} %bitcast.6, f32[12]{0:T(128)} %b2_ref.1, f32[6,8,16,128]{3,2,1,0:T(8,128)} %st_ref.1, ...), custom_call_target="tpu_custom_call" | custom-call | tf_op jit(solution)/shard_map/pallas_call | solution.py:522
  48.6 2.2 %copy.9 = f32[12,8,16,128]{3,2,1,0:T(8,128)} copy(f32[12,8,16,128]{3,1,2,0:T(8,128)} %bitcast.4) | data formatting | bytes 1572864
  50.8 1.8 %copy.10 = f32[6,8,16,128]{3,2,1,0:T(8,128)} copy(f32[6,8,16,128]{3,1,2,0:T(8,128)} %bitcast.5) | data formatting | bytes 786432

commit v4 on v3

--- a/solution.py
+++ b/solution.py
@@ -51,9 +51,9 @@
     return v if s == 0 else pltpu.roll(v, s, v.ndim - 1)
 
 
-def kernel(n_lon, n_lat, x_hbm, w1_ref, b1_ref, w2_ref, b2_ref, st_ref, tab_ref,
+def kernel(n_lon, n_lat, x_hbm, w1_hbm, b1_hbm, w2_hbm, b2_ref, st_hbm, tab_hbm,
            vel_ref, tend_ref,
-           xin, xt, ht, lhs1, lhs2, oh, ohe, bias, xe, xh, xc, pm, pe, fm, fe, pk, pr, rowr, epk, epr,
+           w1_ref, b1_ref, w2_ref, st_ref, tab_ref, arg_sem, xin, xt, ht, lhs1, lhs2, oh, ohe, bias, xe, xh, xc, pm, pe, fm, fe, pk, pr, rowr, epk, epr,
            in_sem, x_s, x_r, row_s, row_r, cor_s, cor_r, lat_s, lat_r, lon_s, lon_r, q_s, q_r):
     lon = lax.axis_index("lon")
     lat = lax.axis_index("lat")
@@ -83,9 +83,26 @@
         pl.semaphore_signal(barrier, inc=1, device_id=north, device_id_type=MESH)
 
     loads = [pltpu.make_async_copy(x_hbm.at[l], xin.at[l], in_sem.at[l]) for l in range(LV)]
-    for c in loads:
+    args = [pltpu.make_async_copy(src, dst, arg_sem.at[i]) for i, (src, dst) in enumerate(
+        ((w1_hbm, w1_ref), (w2_hbm, w2_ref), (b1_hbm, b1_ref), (st_hbm, st_ref), (tab_hbm, tab_ref)))]
+    for c in (*args[:3], *loads, *args[3:]):
         c.start()
 
+    k_id = lax.broadcasted_iota(jnp.int32, (CH, 2 * NY), 0)
+    lane2 = lanes((CH, 2 * NY))
+    half = (k_id // 16) % 2
+    target = half * NY + jnp.where(k_id < 64, 0, NY - 1)
+    hit = lane2 == target
+
+    @pl.loop(0, NX)
+    def _(x):
+        oh[x] = jnp.where(hit & (k_id % 16 == x), 1.0, 0.0).astype(BF16)
+        want_hi = (k_id == NY - 1) & (lane2 == x)
+        want_lo = (k_id == 0) & (lane2 == NY + x)
+        ohe[x] = jnp.where(want_hi | want_lo, 1.0, 0.0).astype(BF16)
+
+    for c in args[:3]:
+        c.wait()
     for b in range(3):
         for a in range(3):
             lhs1[0, b * CH:(b + 1) * CH, a * CH:(a + 1) * CH] = jnp.transpose(w1_ref[a, b], (1, 0))
@@ -100,19 +117,6 @@
                     base = b * 64 + off * 16
                     lhs2[base:base + NC, r * CH:(r + 1) * CH] = w2_ref[a, b]
     bias[...] = jnp.transpose(jnp.broadcast_to(b1_ref[...], (CH, CH)), (1, 0))
-    k_id = lax.broadcasted_iota(jnp.int32, (CH, 2 * NY), 0)
-    lane2 = lanes((CH, 2 * NY))
-    half = (k_id // 16) % 2
-    target = half * NY + jnp.where(k_id < 64, 0, NY - 1)
-    hit = lane2 == target
-
-    @pl.loop(0, NX)
-    def _(x):
-        oh[x] = jnp.where(hit & (k_id % 16 == x), 1.0, 0.0).astype(BF16)
-        want_hi = (k_id == NY - 1) & (lane2 == x)
-        want_lo = (k_id == 0) & (lane2 == NY + x)
-        ohe[x] = jnp.where(want_hi | want_lo, 1.0, 0.0).astype(BF16)
-
     ht[:, 0] = jnp.zeros((LV, CH, NY), BF16)
     ht[:, NX + 1] = jnp.zeros((LV, CH, NY), BF16)
 
@@ -204,6 +208,8 @@
     x_lat = lat_exchange(xe.at[0], xe.at[1], xh.at[0], xh.at[1], x_s, x_r, 0)
 
     zero8 = jnp.zeros((LV, NY), F32)
+    for c in args[3:]:
+        c.wait()
     for v in range(NV):
         fm[NC + v, M:M + NX] = jnp.transpose(st_ref[v], (1, 0, 2))
 
@@ -518,15 +524,24 @@
 
     def body(hidden_in, w1, b1, w2, b2, state):
         vmem = pl.BlockSpec(memory_space=pltpu.VMEM)
+        hbm = pl.BlockSpec(memory_space=pltpu.HBM)
+
+        def keep(array):
+            return pltpu.with_memory_space_constraint(array, pltpu.HBM)
         dma = pltpu.SemaphoreType.DMA
         vel, tend = pl.pallas_call(
             functools.partial(kernel, n_lon, n_lat),
             out_shape=(jax.ShapeDtypeStruct((NC, NX, LV, NY), F32),
                        jax.ShapeDtypeStruct((NV, NX, LV, NY), F32)),
-            in_specs=[pl.BlockSpec(memory_space=pl.ANY), vmem, vmem, vmem,
-                      pl.BlockSpec(memory_space=pltpu.SMEM), vmem, vmem],
+            in_specs=[hbm, hbm, hbm, hbm, pl.BlockSpec(memory_space=pltpu.SMEM), hbm, hbm],
             out_specs=(vmem, vmem),
             scratch_shapes=[
+                pltpu.VMEM(w1.shape, BF16),
+                pltpu.VMEM((1, CH), F32),
+                pltpu.VMEM((3, 3, NC, CH), BF16),
+                pltpu.VMEM((NV, LV, NX, NY), F32),
+                pltpu.VMEM(tables.shape, F32),
+                dma((5,)),
                 pltpu.VMEM((LV, CH, NX, NY), BF16),
                 pltpu.VMEM((LV, NX + 2, CH, NY), BF16),
                 pltpu.VMEM((LV, NX + 2, CH, NY), BF16),
@@ -551,9 +566,9 @@
                 dma((6,)), dma((6,)), dma((6,)), dma((6,)), dma((4,)), dma((4,)),
             ],
             compiler_params=pltpu.CompilerParams(
-                collective_id=0, has_side_effects=True, vmem_limit_bytes=55 * 1024 * 1024),
-        )(hidden_in, w1, b1.reshape(1, CH), jnp.transpose(w2, (0, 1, 3, 2)), b2, state,
-          jnp.asarray(tables))
+                collective_id=0, has_side_effects=True, vmem_limit_bytes=44 * 1024 * 1024),
+        )(keep(hidden_in), keep(w1), keep(b1.reshape(1, CH)), keep(jnp.transpose(w2, (0, 1, 3, 2))), keep(b2),
+          keep(state), keep(jnp.asarray(tables)))
         return jnp.transpose(vel, (0, 2, 1, 3)), jnp.transpose(tend, (0, 2, 1, 3))
 
     spread = P(None, None, "lon", "lat")

time: 52.8 us -> 50.4 us (0.955)
  local copies, waits for them, and re-layouts: 3.96 us -> 1.83 us
    unnamed x2, local copies, waits for them, and re-layouts: 3.96 us -> 1.83 us
where the time goes in v4:
time: 50.4 us; the launch traced here: 50.3 us
  Pallas kernels  47.8 us (95%)
  local copies, waits for them, and re-layouts  1.83 us (4%)
  between operations  0.64 us (1%)
    pallas_call x1, Pallas kernels, body(): pl.pallas_call(functools.partial(kernel, n_lon, n_lat), out_shape=(jax.Sh...  47.8 us
    unnamed x2, local copies, waits for them, and re-layouts  1.83 us

profile of v4, /device:TPU:1, one launch (start us, length us, event | category | flops | bytes accessed | tf_op | source)
XLA Modules:
  0.0 50.3 jit_solution(10182162296921483799)
XLA Ops:
  0.6 47.8 %shard_map.86 = (f32[12,16,8,128]{3,2,1,0:T(8,128)S(1)}, f32[6,16,8,128]{3,2,1,0:T(8,128)S(1)}) custom-call(bf16[8,128,16,128]{3,2,1,0:T(8,128)(2,1)} %x_hbm.1, bf16[3,3,128,128]{3,2,1,0:T(8,128)(2,1)} %w1_hbm.1, f32[1,128]{1,0:T(1,128)} %bitcast.7, bf16[3,3,12,128]{3,2,1,0:T(8,128)(2,1)} %bitcast.6, f32[12]{0:T(128)} %b2_ref.1, f32[6,8,16,128]{3,2,1,0:T(8,128)} %st_hbm.1, ...), custom_call_target="tpu_custom_call" | custom-call | tf_op jit(solution)/shard_map/pallas_call | solution.py:532
  48.5 1.0 %copy.9 = f32[12,8,16,128]{3,2,1,0:T(8,128)} copy(f32[12,8,16,128]{3,1,2,0:T(8,128)S(1)} %bitcast.4) | data formatting | bytes 1572864
  49.5 0.8 %copy.10 = f32[6,8,16,128]{3,2,1,0:T(8,128)} copy(f32[6,8,16,128]{3,1,2,0:T(8,128)S(1)} %bitcast.5) | data formatting | bytes 786432

commit v5 on v4

--- a/solution.py
+++ b/solution.py
@@ -53,7 +53,7 @@
 
 def kernel(n_lon, n_lat, x_hbm, w1_hbm, b1_hbm, w2_hbm, b2_ref, st_hbm, tab_hbm,
            vel_ref, tend_ref,
-           w1_ref, b1_ref, w2_ref, st_ref, tab_ref, arg_sem, xin, xt, ht, lhs1, lhs2, oh, ohe, bias, xe, xh, xc, pm, pe, fm, fe, pk, pr, rowr, epk, epr,
+           w1_ref, b1_ref, w2_ref, st_ref, tab_ref, arg_sem, xin, xt, ht, lhs1, lhs2, oh, ohe, bias, xe, xh, xs, xc, pm, pe, fm, fe, pk, pr, rowr, epk, epr,
            in_sem, x_s, x_r, row_s, row_r, cor_s, cor_r, lat_s, lat_r, lon_s, lon_r, q_s, q_r):
     lon = lax.axis_index("lon")
     lat = lax.axis_index("lat")
@@ -218,8 +218,12 @@
         pack_lat(2 * NC + v, [(fm[NC + v, M + x], zero8) for x in range(NX)])
 
     x_lat()
-    c_left = rcopy(xh, xc.at[1], cor_s.at[0], cor_r.at[0], left)
-    c_right = rcopy(xh, xc.at[0], cor_s.at[1], cor_r.at[1], right)
+    xpos = lanes((CH, NY)) % NX
+    h0, h1 = xh[0].astype(F32), xh[1].astype(F32)
+    xs[0] = jnp.where(xpos == 0, h0, roll(h1, 1)).astype(BF16)
+    xs[1] = jnp.where(xpos == NX - 1, h0, roll(h1, -1)).astype(BF16)
+    c_left = rcopy(xs.at[0], xc.at[1], cor_s.at[0], cor_r.at[0], left)
+    c_right = rcopy(xs.at[1], xc.at[0], cor_s.at[1], cor_r.at[1], right)
     c_left.start()
     c_right.start()
     rows_left[1].start()
@@ -231,15 +235,14 @@
         c.start()
 
     def inject(corners):
-        xpos = lanes((CH, NY)) % NX
         kinds = []
         for side in range(2):
             b = 2 * side
             own = xh[side].astype(F32)
             t0, t2 = roll(own, 1), roll(own, -1)
             if corners:
-                t0 = jnp.where(xpos == 0, roll(xc[0, side].astype(F32), -(NX - 1)), t0)
-                t2 = jnp.where(xpos == NX - 1, roll(xc[1, side].astype(F32), NX - 1), t2)
+                t0 = jnp.where(xpos == 0, roll(xc[0].astype(F32), side - (NX - 1)), t0)
+                t2 = jnp.where(xpos == NX - 1, roll(xc[1].astype(F32), NX - 1 - side), t2)
             taps = jnp.concatenate([t0.astype(BF16), xh[side], t2.astype(BF16)], axis=0)
             e = jnp.dot(lhs1[0, b * CH:(b + 1) * CH, 0:3 * CH], taps, preferred_element_type=F32)
             e_hi = e.astype(BF16).astype(F32)
@@ -552,7 +555,8 @@
                 pltpu.VMEM((CH, NY), F32),
                 pltpu.VMEM((2, CH, NY), BF16),
                 pltpu.VMEM((2, CH, NY), BF16),
-                pltpu.VMEM((2, 2, CH, NY), BF16),
+                pltpu.VMEM((2, CH, NY), BF16),
+                pltpu.VMEM((2, CH, NY), BF16),
                 pltpu.VMEM((NR * NC * LV, NY), F32),
                 pltpu.VMEM((NR * NC * LV, NY), F32),
                 pltpu.VMEM((NF, EX, LV, NY), F32),

time: 50.4 us -> 49.8 us (0.988)
  Pallas kernels: 47.8 us -> 47.2 us
    pallas_call x1, Pallas kernels: 47.8 us -> 47.2 us  [body(): pl.pallas_call(functools.partial(kernel, n_lon, n_lat), out_shape=(jax.Sh...]
where the time goes in v5:
time: 49.8 us; the launch traced here: 49.7 us
  Pallas kernels  47.2 us (95%)
  local copies, waits for them, and re-layouts  1.83 us (4%)
  between operations  0.64 us (1%)
    pallas_call x1, Pallas kernels, body(): pl.pallas_call(functools.partial(kernel, n_lon, n_lat), out_shape=(jax.Sh...  47.2 us
    unnamed x2, local copies, waits for them, and re-layouts  1.83 us

profile of v5, /device:TPU:1, one launch (start us, length us, event | category | flops | bytes accessed | tf_op | source)
XLA Modules:
  0.0 49.7 jit_solution(10622065524226939160)
XLA Ops:
  0.6 47.2 %shard_map.86 = (f32[12,16,8,128]{3,2,1,0:T(8,128)S(1)}, f32[6,16,8,128]{3,2,1,0:T(8,128)S(1)}) custom-call(bf16[8,128,16,128]{3,2,1,0:T(8,128)(2,1)} %x_hbm.1, bf16[3,3,128,128]{3,2,1,0:T(8,128)(2,1)} %w1_hbm.1, f32[1,128]{1,0:T(1,128)} %bitcast.7, bf16[3,3,12,128]{3,2,1,0:T(8,128)(2,1)} %bitcast.6, f32[12]{0:T(128)} %b2_ref.1, f32[6,8,16,128]{3,2,1,0:T(8,128)} %st_hbm.1, ...), custom_call_target="tpu_custom_call" | custom-call | tf_op jit(solution)/shard_map/pallas_call | solution.py:535
  47.8 1.0 %copy.9 = f32[12,8,16,128]{3,2,1,0:T(8,128)} copy(f32[12,8,16,128]{3,1,2,0:T(8,128)S(1)} %bitcast.4) | data formatting | bytes 1572864
  48.8 0.8 %copy.10 = f32[6,8,16,128]{3,2,1,0:T(8,128)} copy(f32[6,8,16,128]{3,1,2,0:T(8,128)S(1)} %bitcast.5) | data formatting | bytes 786432

commit v6 on v5

--- a/solution.py
+++ b/solution.py
@@ -557,8 +557,8 @@
                 pltpu.VMEM((2, CH, NY), BF16),
                 pltpu.VMEM((2, CH, NY), BF16),
                 pltpu.VMEM((2, CH, NY), BF16),
-                pltpu.VMEM((NR * NC * LV, NY), F32),
-                pltpu.VMEM((NR * NC * LV, NY), F32),
+                pltpu.VMEM((NR * NC * LV + 8 * LV, NY), F32),
+                pltpu.VMEM((NR * NC * LV + 8 * LV, NY), F32),
                 pltpu.VMEM((NF, EX, LV, NY), F32),
                 pltpu.VMEM((NF, EX, LV, NY), F32),
                 pltpu.VMEM((2, NP, LV, NY), F32),

time: 49.8 us -> 49.8 us (level)
  no operation moved by 1% of the time
where the time goes in v6:
time: 49.8 us; the launch traced here: 49.7 us
  Pallas kernels  47.2 us (95%)
  local copies, waits for them, and re-layouts  1.83 us (4%)
  between operations  0.64 us (1%)
    pallas_call x1, Pallas kernels, body(): pl.pallas_call(functools.partial(kernel, n_lon, n_lat), out_shape=(jax.Sh...  47.2 us
    unnamed x2, local copies, waits for them, and re-layouts  1.83 us

profile of v6, /device:TPU:1, one launch (start us, length us, event | category | flops | bytes accessed | tf_op | source)
XLA Modules:
  0.0 49.7 jit_solution(10248612378678375065)
XLA Ops:
  0.6 47.2 %shard_map.86 = (f32[12,16,8,128]{3,2,1,0:T(8,128)S(1)}, f32[6,16,8,128]{3,2,1,0:T(8,128)S(1)}) custom-call(bf16[8,128,16,128]{3,2,1,0:T(8,128)(2,1)} %x_hbm.1, bf16[3,3,128,128]{3,2,1,0:T(8,128)(2,1)} %w1_hbm.1, f32[1,128]{1,0:T(1,128)} %bitcast.7, bf16[3,3,12,128]{3,2,1,0:T(8,128)(2,1)} %bitcast.6, f32[12]{0:T(128)} %b2_ref.1, f32[6,8,16,128]{3,2,1,0:T(8,128)} %st_hbm.1, ...), custom_call_target="tpu_custom_call" | custom-call | tf_op jit(solution)/shard_map/pallas_call | solution.py:535
  47.8 1.0 %copy.9 = f32[12,8,16,128]{3,2,1,0:T(8,128)} copy(f32[12,8,16,128]{3,1,2,0:T(8,128)S(1)} %bitcast.4) | data formatting | bytes 1572864
  48.8 0.8 %copy.10 = f32[6,8,16,128]{3,2,1,0:T(8,128)} copy(f32[6,8,16,128]{3,1,2,0:T(8,128)S(1)} %bitcast.5) | data formatting | bytes 786432
